TPU v7x, 32 devices: a whole 2x2x4 slice. The times are simulated.
32 devices in a mesh: bx: 4 (over y, x), by: 8 (over z, core).
Axes of the slice: x: 2, y: 2, z: 4, core: 2. Of those that a mesh axis runs over, the one named last changes fastest.
Arguments:
- terminal_value: float32 [64, 128, 256], P('bx', 'by'), may hold values from -3 to 3
- density: float32 [64, 128, 256], P('bx', 'by')
- potential: float32 [64, 128, 256], P('bx', 'by'), may hold values from -5 to 5
- heights: int32 [64, 128], P('bx', 'by'), may hold values from 0 to 64
Outputs:
- value_field: float32 [64, 128, 256], P('bx', 'by')
- density_next: float32 [64, 128, 256], P('bx', 'by')
All inputs are finite; a program needn't handle non-finite values.
Results may differ from a plain program's by a relative error of at most 0.0001.
Values sent between devices are 32-bit elements; how exact they have to be, the bound alone decides.
A program may use at most 64 MiB of HBM per device.

v0:
```python
import jax
import jax.numpy as jnp
from jax import lax
from jax.sharding import PartitionSpec as P

ITERS = 3


DT_HJB = 0.5
NU_HJB = 0.25
COUPLE = 0.5
PENALTY = 2.0
DT_FP = 0.25
DIFFUSE = 1.0
ABSORB = 4.0


def extended(x, sides, width):
    for axis, dim in sides:
        peers, length = (lax.axis_size(axis), x.shape[dim])
        up = [(i, (i + 1) % peers) for i in range(peers - 1)]
        down = [(j, i) for i, j in up]
        last = lax.slice_in_dim(x, length - width, length, axis=dim)
        first = lax.slice_in_dim(x, 0, width, axis=dim)
        before = lax.ppermute(last, axis, up)
        after = lax.ppermute(first, axis, down)
        x = jnp.concatenate([before, x, after], axis=dim)
    return x


def neighbours(padded):
    full = jnp.pad(padded, ((0, 0), (0, 0), (1, 1)))
    centre = full[1:-1, 1:-1, 1:-1]
    pairs = [
        (full[2:, 1:-1, 1:-1], full[:-2, 1:-1, 1:-1]),
        (full[1:-1, 2:, 1:-1], full[1:-1, :-2, 1:-1]),
        (full[1:-1, 1:-1, 2:], full[1:-1, 1:-1, :-2]),
    ]
    return (centre, pairs)


def hjb_update(padded, cost):
    centre, pairs = neighbours(padded)
    laplace = -6.0 * centre
    hamilton = jnp.zeros_like(centre)
    for upper, lower in pairs:
        laplace = laplace + upper + lower
        hamilton = (
            hamilton
            + jnp.square(jnp.maximum(centre - lower, 0.0))
            + jnp.square(jnp.minimum(upper - centre, 0.0))
        )
    return centre + DT_HJB * (NU_HJB * laplace - 0.5 * hamilton + cost)


def transport(mass_pad, value_pad):
    mass, mass_pairs = neighbours(mass_pad)
    value, value_pairs = neighbours(value_pad)
    divergence = jnp.zeros_like(mass)
    for mass_side, value_side in zip(mass_pairs, value_pairs):
        mass_up, mass_low = mass_side
        value_up, value_low = value_side
        speed_up = value - value_up
        flux_up = jnp.maximum(speed_up, 0.0) * mass + jnp.minimum(speed_up, 0.0) * mass_up
        speed_low = value_low - value
        flux_low = jnp.maximum(speed_low, 0.0) * mass_low + jnp.minimum(speed_low, 0.0) * mass
        divergence = divergence + (flux_up - flux_low)
    return mass - DT_FP * divergence


def apply_operator(field, diagonal):
    padded = extended(field, (("bx", 0), ("by", 1)), 1)
    centre, pairs = neighbours(padded)
    total = jnp.zeros_like(centre)
    for upper, lower in pairs:
        total = total + upper + lower
    return diagonal * centre - DIFFUSE * total


def value_step(field, cost):
    padded = extended(field, (("bx", 0), ("by", 1)), 1)
    return hjb_update(padded, cost)


def residual_squares(residual):
    return lax.psum(jnp.sum(residual * residual), ("bx", "by"))


def per_device(terminal_value, density, potential, heights):
    cells_x, cells_y, depth = terminal_value.shape
    levels = lax.broadcasted_iota(jnp.int32, (1, 1, depth), 2)
    blocked = (levels < heights[:, :, None]).astype(jnp.float32)
    cost = potential + COUPLE * density + PENALTY * blocked
    value_mid = value_step(terminal_value, cost)
    value_field = value_step(value_mid, cost)
    joined = extended(jnp.stack([density, value_field]), (("bx", 1), ("by", 2)), 1)
    target = transport(joined[0], joined[1])
    diagonal = 1.0 + 6.0 * DIFFUSE + ABSORB * blocked
    solution = target
    residual = target - apply_operator(target, diagonal)
    direction = residual
    norm_now = residual_squares(residual)
    for iteration in range(ITERS):
        image = apply_operator(direction, diagonal)
        alpha = norm_now / lax.psum(jnp.sum(direction * image), ("bx", "by"))
        solution = solution + alpha * direction
        residual = residual - alpha * image
        norm_next = residual_squares(residual)
        direction = residual + norm_next / norm_now * direction
        norm_now = norm_next
    return (value_field, solution)


def solution(mesh):
    return jax.shard_map(
        per_device,
        mesh=mesh,
        in_specs=(P("bx", "by", None), P("bx", "by", None), P("bx", "by", None), P("bx", "by")),
        out_specs=(P("bx", "by", None), P("bx", "by", None)),
        check_vma=False,
    )
```

profile of v0, /device:TPU:0, one launch (start us, length us, event | category | flops | bytes accessed | tf_op | source)
XLA Modules:
  0.0 338.0 jit_solution(2207830926272911994)
XLA Ops:
  0.6 0.7 fusion.91
  1.4 4.9 %collective-permute-start.1 = (f32[1,16,256]{2,1,0:T(8,128)S(1)}, f32[1,16,256]{2,1,0:T(8,128)S(1)}, u32[]{:S(2)}, u32[]{:S(2)}) collective-permute-start(f32[1,16,256]{2,1,0:T(8,128)S(1)} %get-tuple-element.40), channel_id=1, source_target_pairs={{0,8},{8,16},{16,24},{1,9},{9,17},{17,25},{2,10},{10,18},{18,26},{... | collective-permute-start | bytes 49160 | tf_op jit(solution)/shard_map/ppermute | solution.py:25
  6.2 1.3 collective-permute-start
  7.7 1.0 constant_dynamic-update-slice_fusion.1
  8.6 3.2 collective-permute-done
  11.9 1.3 collective-permute-start.3
  13.3 1.4 collective-permute-start.2
  14.7 3.6 %collective-permute-done.2 = f32[18,1,256]{2,1,0:T(1,128)S(1)} collective-permute-done((f32[18,1,256]{2,1,0:T(1,128)S(1)}, f32[18,1,256]{2,1,0:T(1,128)S(1)}, u32[]{:S(2)}, u32[]{:S(2)}) %collective-permute-start.2) | collective-permute-done | bytes 18464 | tf_op jit(solution)/shard_map/ppermute | solution.py:26
  18.3 0.4 select_maximum_fusion.20
  18.7 0.5 fusion.73
  19.2 1.3 collective-permute-start.4
  20.5 4.9 %collective-permute-start.5 = (f32[1,16,256]{2,1,0:T(8,128)S(1)}, f32[1,16,256]{2,1,0:T(8,128)S(1)}, u32[]{:S(2)}, u32[]{:S(2)}) collective-permute-start(f32[1,16,256]{2,1,0:T(8,128)S(1)} %get-tuple-element.38), channel_id=1, source_target_pairs={{0,8},{8,16},{16,24},{1,9},{9,17},{17,25},{2,10},{10,18},{18,26},{... | collective-permute-start | bytes 49160 | tf_op jit(solution)/shard_map/ppermute | solution.py:25
  25.5 1.4 collective-permute-done.5
  26.9 3.5 %collective-permute-start.7 = (f32[18,1,256]{2,1,0:T(1,128)S(1)}, f32[18,1,256]{2,1,0:T(1,128)S(1)}, u32[]{:S(2)}, u32[]{:S(2)}) collective-permute-start(f32[18,1,256]{2,1,0:T(1,128)S(1)} %get-tuple-element.25), channel_id=1, source_target_pairs={{0,1},{1,2},{2,3},{3,4},{4,5},{5,6},{6,7},{8,9},{9,10},{10,11},{11... | collective-permute-start | bytes 55304 | tf_op jit(solution)/shard_map/ppermute | solution.py:25
  30.5 1.3 collective-permute-start.6
  31.8 2.2 collective-permute-done.6
  33.9 0.4 select_maximum_fusion.16
  34.3 0.5 fusion.50
  34.8 4.8 %collective-permute-start.8 = (f32[2,1,16,256]{3,2,1,0:T(8,128)S(1)}, f32[2,1,16,256]{3,2,1,0:T(8,128)S(1)}, u32[]{:S(2)}, u32[]{:S(2)}) collective-permute-start(f32[2,1,16,256]{3,2,1,0:T(8,128)S(1)} %get-tuple-element.15), channel_id=1, source_target_pairs={{0,8},{8,16},{16,24},{1,9},{9,17},{17,25},{2,10},{10,18},{18,26},{... | collective-permute-start | bytes 98312 | tf_op jit(solution)/shard_map/ppermute | solution.py:25
  39.6 1.3 collective-permute-start.9
  41.2 5.4 %collective-permute-done.9 = f32[2,1,16,256]{3,2,1,0:T(8,128)S(1)} collective-permute-done((f32[2,1,16,256]{3,2,1,0:T(8,128)S(1)}, f32[2,1,16,256]{3,2,1,0:T(8,128)S(1)}, u32[]{:S(2)}, u32[]{:S(2)}) %collective-permute-start.9) | collective-permute-done | bytes 32800 | tf_op jit(solution)/shard_map/ppermute | solution.py:26
  46.7 3.3 collective-permute-start.10
  50.0 1.3 collective-permute-start.11
  51.3 2.5 collective-permute-done.11
  54.0 0.5 fusion.8
  54.5 4.8 %collective-permute-start.13 = (f32[1,16,256]{2,1,0:T(8,128)S(1)}, f32[1,16,256]{2,1,0:T(8,128)S(1)}, u32[]{:S(2)}, u32[]{:S(2)}) collective-permute-start(f32[1,16,256]{2,1,0:T(8,128)S(1)} %get-tuple-element.35), channel_id=1, source_target_pairs={{0,8},{8,16},{16,24},{1,9},{9,17},{17,25},{2,10},{10,18},{18,26},{... | collective-permute-start | bytes 49160 | tf_op jit(solution)/shard_map/ppermute | solution.py:25
  59.3 1.3 collective-permute-start.12
  60.7 4.2 %collective-permute-done.12 = f32[1,16,256]{2,1,0:T(8,128)S(1)} collective-permute-done((f32[1,16,256]{2,1,0:T(8,128)S(1)}, f32[1,16,256]{2,1,0:T(8,128)S(1)}, u32[]{:S(2)}, u32[]{:S(2)}) %collective-permute-start.12) | collective-permute-done | bytes 16416 | tf_op jit(solution)/shard_map/ppermute | solution.py:26
  65.0 3.1 collective-permute-start.15
  68.1 1.3 collective-permute-start.14
  69.4 2.7 collective-permute-done.14
  72.1 0.4 select_maximum_fusion.12
  72.8 2.8 collective-permute-start.17
  75.6 1.3 collective-permute-start.16
  77.0 4.2 %collective-permute-done.16 = f32[1,16,256]{2,1,0:T(8,128)S(1)} collective-permute-done((f32[1,16,256]{2,1,0:T(8,128)S(1)}, f32[1,16,256]{2,1,0:T(8,128)S(1)}, u32[]{:S(2)}, u32[]{:S(2)}) %collective-permute-start.16) | collective-permute-done | bytes 16416 | tf_op jit(solution)/shard_map/ppermute | solution.py:26
  81.3 3.0 collective-permute-start.19
  84.2 1.3 collective-permute-start.18
  85.6 2.7 collective-permute-done.18
  88.3 0.4 select_maximum_fusion.8
  88.7 0.9 multiply_reduce_fusion.3
  89.6 41.1 %all-reduce.8 = (f32[]{:T(128)}, f32[]{:T(128)}) all-reduce(f32[]{:T(128)} %get-tuple-element.3, f32[]{:T(128)} %get-tuple-element.2), channel_id=1, replica_groups=mesh['bx'=4,'by'=8] {'bx','by'}, use_global_device_ids=true, to_apply=%region_1.2 | all-reduce | flops 2 | bytes 16 | tf_op jit(solution)/shard_map/psum | solution.py:86
  131.9 0.7 multiply_reduce_fusion.2
  132.6 40.2 %psum.44 = f32[]{:T(128)} all-reduce(f32[]{:T(128)} %get-tuple-element.8), channel_id=1, replica_groups=mesh['bx'=4,'by'=8] {'bx','by'}, use_global_device_ids=true, to_apply=%region_5.6 | all-reduce | flops 1 | bytes 8 | tf_op jit(solution)/shard_map/psum | solution.py:86
  174.1 4.2 %collective-permute-start.21 = (f32[1,16,256]{2,1,0:T(8,128)S(1)}, f32[1,16,256]{2,1,0:T(8,128)S(1)}, u32[]{:S(2)}, u32[]{:S(2)}) collective-permute-start(f32[1,16,256]{2,1,0:T(8,128)S(1)} %get-tuple-element.31), channel_id=1, source_target_pairs={{0,8},{8,16},{16,24},{1,9},{9,17},{17,25},{2,10},{10,18},{18,26},{... | collective-permute-start | bytes 49160 | tf_op jit(solution)/shard_map/ppermute | solution.py:25
  178.3 1.3 collective-permute-start.20
  179.7 4.2 %collective-permute-done.20 = f32[1,16,256]{2,1,0:T(8,128)S(1)} collective-permute-done((f32[1,16,256]{2,1,0:T(8,128)S(1)}, f32[1,16,256]{2,1,0:T(8,128)S(1)}, u32[]{:S(2)}, u32[]{:S(2)}) %collective-permute-start.20) | collective-permute-done | bytes 16416 | tf_op jit(solution)/shard_map/ppermute | solution.py:26
  184.0 1.3 collective-permute-start.23
  185.3 1.3 collective-permute-start.22
  186.6 3.2 collective-permute-done.22
  189.8 0.4 select_maximum_fusion.4
  190.2 0.9 multiply_reduce_fusion.1
  191.1 42.3 %psum.45 = f32[]{:T(128)} all-reduce(f32[]{:T(128)} %get-tuple-element.6), channel_id=1, replica_groups=mesh['bx'=4,'by'=8] {'bx','by'}, use_global_device_ids=true, to_apply=%region_7.8 | all-reduce | flops 1 | bytes 8 | tf_op jit(solution)/shard_map/psum | solution.py:105
  234.6 0.7 multiply_reduce_fusion
  235.4 39.7 %psum.46 = f32[]{:T(128)} all-reduce(f32[]{:T(128)} %multiply_reduce_fusion), channel_id=1, replica_groups=mesh['bx'=4,'by'=8] {'bx','by'}, use_global_device_ids=true, to_apply=%region_9.10 | all-reduce | flops 1 | bytes 8 | tf_op jit(solution)/shard_map/psum | solution.py:86
  276.5 4.2 %collective-permute-start.25 = (f32[1,16,256]{2,1,0:T(8,128)S(1)}, f32[1,16,256]{2,1,0:T(8,128)S(1)}, u32[]{:S(2)}, u32[]{:S(2)}) collective-permute-start(f32[1,16,256]{2,1,0:T(8,128)S(1)} %get-tuple-element.29), channel_id=1, source_target_pairs={{0,8},{8,16},{16,24},{1,9},{9,17},{17,25},{2,10},{10,18},{18,26},{... | collective-permute-start | bytes 49160 | tf_op jit(solution)/shard_map/ppermute | solution.py:25
  280.7 1.3 collective-permute-start.24
  282.1 4.2 %collective-permute-done.24 = f32[1,16,256]{2,1,0:T(8,128)S(1)} collective-permute-done((f32[1,16,256]{2,1,0:T(8,128)S(1)}, f32[1,16,256]{2,1,0:T(8,128)S(1)}, u32[]{:S(2)}, u32[]{:S(2)}) %collective-permute-start.24) | collective-permute-done | bytes 16416 | tf_op jit(solution)/shard_map/ppermute | solution.py:26
  286.4 1.3 collective-permute-start.27
  287.7 1.3 collective-permute-start.26
  289.0 3.2 collective-permute-done.26
  292.2 0.4 select_maximum_fusion
  292.6 0.9 fusion.13
  293.5 42.3 %psum.47 = f32[]{:T(128)} all-reduce(f32[]{:T(128)} %fusion.13), channel_id=1, replica_groups=mesh['bx'=4,'by'=8] {'bx','by'}, use_global_device_ids=true, to_apply=%region_11.12 | all-reduce | flops 1 | bytes 8 | tf_op jit(solution)/shard_map/psum | solution.py:105
  337.1 0.8 multiply_add_fusion
  (44 shorter events, 1.8 us)
Async XLA Ops:
  1.4 6.3 %collective-permute-start.1 = (f32[1,16,256]{2,1,0:T(8,128)S(1)}, f32[1,16,256]{2,1,0:T(8,128)S(1)}, u32[]{:S(2)}, u32[]{:S(2)}) collective-permute-start(f32[1,16,256]{2,1,0:T(8,128)S(1)} %get-tuple-element.40), channel_id=1, source_target_pairs={{0,8},{8,16},{16,24},{1,9},{9,17},{17,25},{2,10},{10,18},{18,26},{... | collective-permute-start | bytes 49160 | tf_op jit(solution)/shard_map/ppermute | solution.py:25
  6.2 5.6 %collective-permute-start = (f32[1,16,256]{2,1,0:T(8,128)S(1)}, f32[1,16,256]{2,1,0:T(8,128)S(1)}, u32[]{:S(2)}, u32[]{:S(2)}) collective-permute-start(f32[1,16,256]{2,1,0:T(8,128)S(1)} %get-tuple-element.39), channel_id=1, source_target_pairs={{8,0},{16,8},{24,16},{9,1},{17,9},{25,17},{10,2},{18,10},{26,18},{... | collective-permute-start | bytes 49160 | tf_op jit(solution)/shard_map/ppermute | solution.py:26
  11.9 2.8 collective-permute-start.3
  13.2 5.5 %copy-start = (f32[16,16,256]{2,1,0:T(8,128)S(1)}, f32[16,16,256]{2,1,0:T(8,128)}, u32[]{:S(2)}) copy-start(f32[16,16,256]{2,1,0:T(8,128)} %param.5) | copy-start | bytes 786436
  13.2 5.5 %copy-start.2 = (f32[16,16,256]{2,1,0:T(8,128)S(1)}, f32[16,16,256]{2,1,0:T(8,128)}, u32[]{:S(2)}) copy-start(f32[16,16,256]{2,1,0:T(8,128)} %param.4) | copy-start | bytes 786436
  13.2 5.4 %copy-start.3 = (f32[16,16,256]{2,1,0:T(8,128)S(1)}, f32[16,16,256]{2,1,0:T(8,128)}, u32[]{:S(2)}) copy-start(f32[16,16,256]{2,1,0:T(8,128)} %param.6) | copy-start | bytes 786436
  13.2 5.4 %copy-start.4 = (s32[16,16]{1,0:T(8,128)S(1)}, s32[16,16]{1,0:T(8,128)}, u32[]{:S(2)}) copy-start(s32[16,16]{1,0:T(8,128)} %param.7) | copy-start | bytes 3076
  13.3 5.0 %collective-permute-start.2 = (f32[18,1,256]{2,1,0:T(1,128)S(1)}, f32[18,1,256]{2,1,0:T(1,128)S(1)}, u32[]{:S(2)}, u32[]{:S(2)}) collective-permute-start(f32[18,1,256]{2,1,0:T(1,128)S(1)} %get-tuple-element.28), channel_id=1, source_target_pairs={{1,0},{2,1},{3,2},{4,3},{5,4},{6,5},{7,6},{9,8},{10,9},{11,10},{12... | collective-permute-start | bytes 55304 | tf_op jit(solution)/shard_map/ppermute | solution.py:26
  19.2 6.2 %collective-permute-start.4 = (f32[1,16,256]{2,1,0:T(8,128)S(1)}, f32[1,16,256]{2,1,0:T(8,128)S(1)}, u32[]{:S(2)}, u32[]{:S(2)}) collective-permute-start(f32[1,16,256]{2,1,0:T(8,128)S(1)} %get-tuple-element.37), channel_id=1, source_target_pairs={{8,0},{16,8},{24,16},{9,1},{17,9},{25,17},{10,2},{18,10},{26,18},{... | collective-permute-start | bytes 49160 | tf_op jit(solution)/shard_map/ppermute | solution.py:26
  20.5 6.4 %collective-permute-start.5 = (f32[1,16,256]{2,1,0:T(8,128)S(1)}, f32[1,16,256]{2,1,0:T(8,128)S(1)}, u32[]{:S(2)}, u32[]{:S(2)}) collective-permute-start(f32[1,16,256]{2,1,0:T(8,128)S(1)} %get-tuple-element.38), channel_id=1, source_target_pairs={{0,8},{8,16},{16,24},{1,9},{9,17},{17,25},{2,10},{10,18},{18,26},{... | collective-permute-start | bytes 49160 | tf_op jit(solution)/shard_map/ppermute | solution.py:25
  26.9 4.9 %collective-permute-start.7 = (f32[18,1,256]{2,1,0:T(1,128)S(1)}, f32[18,1,256]{2,1,0:T(1,128)S(1)}, u32[]{:S(2)}, u32[]{:S(2)}) collective-permute-start(f32[18,1,256]{2,1,0:T(1,128)S(1)} %get-tuple-element.25), channel_id=1, source_target_pairs={{0,1},{1,2},{2,3},{3,4},{4,5},{5,6},{6,7},{8,9},{9,10},{10,11},{11... | collective-permute-start | bytes 55304 | tf_op jit(solution)/shard_map/ppermute | solution.py:25
  30.5 3.5 %collective-permute-start.6 = (f32[18,1,256]{2,1,0:T(1,128)S(1)}, f32[18,1,256]{2,1,0:T(1,128)S(1)}, u32[]{:S(2)}, u32[]{:S(2)}) collective-permute-start(f32[18,1,256]{2,1,0:T(1,128)S(1)} %get-tuple-element.26), channel_id=1, source_target_pairs={{1,0},{2,1},{3,2},{4,3},{5,4},{6,5},{7,6},{9,8},{10,9},{11,10},{12... | collective-permute-start | bytes 55304 | tf_op jit(solution)/shard_map/ppermute | solution.py:26
  34.8 19.0 %copy-start.1 = (f32[16,16,256]{2,1,0:T(8,128)}, f32[16,16,256]{2,1,0:T(8,128)S(1)}, u32[]{:S(2)}) copy-start(f32[16,16,256]{2,1,0:T(8,128)S(1)} %fusion.50) | copy-start | bytes 786436
  34.8 6.4 %collective-permute-start.8 = (f32[2,1,16,256]{3,2,1,0:T(8,128)S(1)}, f32[2,1,16,256]{3,2,1,0:T(8,128)S(1)}, u32[]{:S(2)}, u32[]{:S(2)}) collective-permute-start(f32[2,1,16,256]{3,2,1,0:T(8,128)S(1)} %get-tuple-element.15), channel_id=1, source_target_pairs={{0,8},{8,16},{16,24},{1,9},{9,17},{17,25},{2,10},{10,18},{18,26},{... | collective-permute-start | bytes 98312 | tf_op jit(solution)/shard_map/ppermute | solution.py:25
  39.6 7.0 %collective-permute-start.9 = (f32[2,1,16,256]{3,2,1,0:T(8,128)S(1)}, f32[2,1,16,256]{3,2,1,0:T(8,128)S(1)}, u32[]{:S(2)}, u32[]{:S(2)}) collective-permute-start(f32[2,1,16,256]{3,2,1,0:T(8,128)S(1)} %get-tuple-element.16), channel_id=1, source_target_pairs={{8,0},{16,8},{24,16},{9,1},{17,9},{25,17},{10,2},{18,10},{26,18},{... | collective-permute-start | bytes 98312 | tf_op jit(solution)/shard_map/ppermute | solution.py:26
  46.7 4.6 %collective-permute-start.10 = (f32[2,18,1,256]{3,2,1,0:T(1,128)S(1)}, f32[2,18,1,256]{3,2,1,0:T(1,128)S(1)}, u32[]{:S(2)}, u32[]{:S(2)}) collective-permute-start(f32[2,18,1,256]{3,2,1,0:T(1,128)S(1)} %get-tuple-element.13), channel_id=1, source_target_pairs={{0,1},{1,2},{2,3},{3,4},{4,5},{5,6},{6,7},{8,9},{9,10},{10,11},{11... | collective-permute-start | bytes 110600 | tf_op jit(solution)/shard_map/ppermute | solution.py:25
  50.0 3.8 %collective-permute-start.11 = (f32[2,18,1,256]{3,2,1,0:T(1,128)S(1)}, f32[2,18,1,256]{3,2,1,0:T(1,128)S(1)}, u32[]{:S(2)}, u32[]{:S(2)}) collective-permute-start(f32[2,18,1,256]{3,2,1,0:T(1,128)S(1)} %get-tuple-element.14), channel_id=1, source_target_pairs={{1,0},{2,1},{3,2},{4,3},{5,4},{6,5},{7,6},{9,8},{10,9},{11,10},{12... | collective-permute-start | bytes 110600 | tf_op jit(solution)/shard_map/ppermute | solution.py:26
  54.5 6.3 %collective-permute-start.13 = (f32[1,16,256]{2,1,0:T(8,128)S(1)}, f32[1,16,256]{2,1,0:T(8,128)S(1)}, u32[]{:S(2)}, u32[]{:S(2)}) collective-permute-start(f32[1,16,256]{2,1,0:T(8,128)S(1)} %get-tuple-element.35), channel_id=1, source_target_pairs={{0,8},{8,16},{16,24},{1,9},{9,17},{17,25},{2,10},{10,18},{18,26},{... | collective-permute-start | bytes 49160 | tf_op jit(solution)/shard_map/ppermute | solution.py:25
  59.3 5.6 %collective-permute-start.12 = (f32[1,16,256]{2,1,0:T(8,128)S(1)}, f32[1,16,256]{2,1,0:T(8,128)S(1)}, u32[]{:S(2)}, u32[]{:S(2)}) collective-permute-start(f32[1,16,256]{2,1,0:T(8,128)S(1)} %get-tuple-element.36), channel_id=1, source_target_pairs={{8,0},{16,8},{24,16},{9,1},{17,9},{25,17},{10,2},{18,10},{26,18},{... | collective-permute-start | bytes 49160 | tf_op jit(solution)/shard_map/ppermute | solution.py:26
  65.0 4.5 %collective-permute-start.15 = (f32[18,1,256]{2,1,0:T(1,128)S(1)}, f32[18,1,256]{2,1,0:T(1,128)S(1)}, u32[]{:S(2)}, u32[]{:S(2)}) collective-permute-start(f32[18,1,256]{2,1,0:T(1,128)S(1)} %get-tuple-element.23), channel_id=1, source_target_pairs={{0,1},{1,2},{2,3},{3,4},{4,5},{5,6},{6,7},{8,9},{9,10},{10,11},{11... | collective-permute-start | bytes 55304 | tf_op jit(solution)/shard_map/ppermute | solution.py:25
  68.1 4.0 %collective-permute-start.14 = (f32[18,1,256]{2,1,0:T(1,128)S(1)}, f32[18,1,256]{2,1,0:T(1,128)S(1)}, u32[]{:S(2)}, u32[]{:S(2)}) collective-permute-start(f32[18,1,256]{2,1,0:T(1,128)S(1)} %get-tuple-element.24), channel_id=1, source_target_pairs={{1,0},{2,1},{3,2},{4,3},{5,4},{6,5},{7,6},{9,8},{10,9},{11,10},{12... | collective-permute-start | bytes 55304 | tf_op jit(solution)/shard_map/ppermute | solution.py:26
  72.8 4.3 %collective-permute-start.17 = (f32[1,16,256]{2,1,0:T(8,128)S(1)}, f32[1,16,256]{2,1,0:T(8,128)S(1)}, u32[]{:S(2)}, u32[]{:S(2)}) collective-permute-start(f32[1,16,256]{2,1,0:T(8,128)S(1)} %get-tuple-element.33), channel_id=1, source_target_pairs={{0,8},{8,16},{16,24},{1,9},{9,17},{17,25},{2,10},{10,18},{18,26},{... | collective-permute-start | bytes 49160 | tf_op jit(solution)/shard_map/ppermute | solution.py:25
  75.6 5.6 %collective-permute-start.16 = (f32[1,16,256]{2,1,0:T(8,128)S(1)}, f32[1,16,256]{2,1,0:T(8,128)S(1)}, u32[]{:S(2)}, u32[]{:S(2)}) collective-permute-start(f32[1,16,256]{2,1,0:T(8,128)S(1)} %get-tuple-element.34), channel_id=1, source_target_pairs={{8,0},{16,8},{24,16},{9,1},{17,9},{25,17},{10,2},{18,10},{26,18},{... | collective-permute-start | bytes 49160 | tf_op jit(solution)/shard_map/ppermute | solution.py:26
  81.3 4.3 %collective-permute-start.19 = (f32[18,1,256]{2,1,0:T(1,128)S(1)}, f32[18,1,256]{2,1,0:T(1,128)S(1)}, u32[]{:S(2)}, u32[]{:S(2)}) collective-permute-start(f32[18,1,256]{2,1,0:T(1,128)S(1)} %get-tuple-element.21), channel_id=1, source_target_pairs={{0,1},{1,2},{2,3},{3,4},{4,5},{5,6},{6,7},{8,9},{9,10},{10,11},{11... | collective-permute-start | bytes 55304 | tf_op jit(solution)/shard_map/ppermute | solution.py:25
  84.2 4.0 %collective-permute-start.18 = (f32[18,1,256]{2,1,0:T(1,128)S(1)}, f32[18,1,256]{2,1,0:T(1,128)S(1)}, u32[]{:S(2)}, u32[]{:S(2)}) collective-permute-start(f32[18,1,256]{2,1,0:T(1,128)S(1)} %get-tuple-element.22), channel_id=1, source_target_pairs={{1,0},{2,1},{3,2},{4,3},{5,4},{6,5},{7,6},{9,8},{10,9},{11,10},{12... | collective-permute-start | bytes 55304 | tf_op jit(solution)/shard_map/ppermute | solution.py:26
  174.1 5.6 %collective-permute-start.21 = (f32[1,16,256]{2,1,0:T(8,128)S(1)}, f32[1,16,256]{2,1,0:T(8,128)S(1)}, u32[]{:S(2)}, u32[]{:S(2)}) collective-permute-start(f32[1,16,256]{2,1,0:T(8,128)S(1)} %get-tuple-element.31), channel_id=1, source_target_pairs={{0,8},{8,16},{16,24},{1,9},{9,17},{17,25},{2,10},{10,18},{18,26},{... | collective-permute-start | bytes 49160 | tf_op jit(solution)/shard_map/ppermute | solution.py:25
  178.3 5.6 %collective-permute-start.20 = (f32[1,16,256]{2,1,0:T(8,128)S(1)}, f32[1,16,256]{2,1,0:T(8,128)S(1)}, u32[]{:S(2)}, u32[]{:S(2)}) collective-permute-start(f32[1,16,256]{2,1,0:T(8,128)S(1)} %get-tuple-element.32), channel_id=1, source_target_pairs={{8,0},{16,8},{24,16},{9,1},{17,9},{25,17},{10,2},{18,10},{26,18},{... | collective-permute-start | bytes 49160 | tf_op jit(solution)/shard_map/ppermute | solution.py:26
  184.0 2.6 collective-permute-start.23
  185.3 4.5 %collective-permute-start.22 = (f32[18,1,256]{2,1,0:T(1,128)S(1)}, f32[18,1,256]{2,1,0:T(1,128)S(1)}, u32[]{:S(2)}, u32[]{:S(2)}) collective-permute-start(f32[18,1,256]{2,1,0:T(1,128)S(1)} %get-tuple-element.20), channel_id=1, source_target_pairs={{1,0},{2,1},{3,2},{4,3},{5,4},{6,5},{7,6},{9,8},{10,9},{11,10},{12... | collective-permute-start | bytes 55304 | tf_op jit(solution)/shard_map/ppermute | solution.py:26
  276.5 5.6 %collective-permute-start.25 = (f32[1,16,256]{2,1,0:T(8,128)S(1)}, f32[1,16,256]{2,1,0:T(8,128)S(1)}, u32[]{:S(2)}, u32[]{:S(2)}) collective-permute-start(f32[1,16,256]{2,1,0:T(8,128)S(1)} %get-tuple-element.29), channel_id=1, source_target_pairs={{0,8},{8,16},{16,24},{1,9},{9,17},{17,25},{2,10},{10,18},{18,26},{... | collective-permute-start | bytes 49160 | tf_op jit(solution)/shard_map/ppermute | solution.py:25
  280.7 5.6 %collective-permute-start.24 = (f32[1,16,256]{2,1,0:T(8,128)S(1)}, f32[1,16,256]{2,1,0:T(8,128)S(1)}, u32[]{:S(2)}, u32[]{:S(2)}) collective-permute-start(f32[1,16,256]{2,1,0:T(8,128)S(1)} %get-tuple-element.30), channel_id=1, source_target_pairs={{8,0},{16,8},{24,16},{9,1},{17,9},{25,17},{10,2},{18,10},{26,18},{... | collective-permute-start | bytes 49160 | tf_op jit(solution)/shard_map/ppermute | solution.py:26
  286.4 2.6 collective-permute-start.27
  287.7 4.6 %collective-permute-start.26 = (f32[18,1,256]{2,1,0:T(1,128)S(1)}, f32[18,1,256]{2,1,0:T(1,128)S(1)}, u32[]{:S(2)}, u32[]{:S(2)}) collective-permute-start(f32[18,1,256]{2,1,0:T(1,128)S(1)} %get-tuple-element.18), channel_id=1, source_target_pairs={{1,0},{2,1},{3,2},{4,3},{5,4},{6,5},{7,6},{9,8},{10,9},{11,10},{12... | collective-permute-start | bytes 55304 | tf_op jit(solution)/shard_map/ppermute | solution.py:26
where the time goes:
time: 340 us; the launch traced here: 338 us
  blocking collectives  206 us (61%)
  starting transfers between devices  65.6 us (19%)
  waiting for transfers between devices  47.9 us (14%)
  other arithmetic  9.39 us (3%)
  between operations  7.67 us (2%)
    psum x3, blocking collectives, residual_squares(): return lax.psum(jnp.sum(residual * residual), ('bx', 'by'))  121 us
    psum x2, blocking collectives, per_device(): alpha = norm_now / lax.psum(jnp.sum(direction * image), ('bx', 'by'))  84.5 us
    ppermute x14, starting transfers between devices, extended(): before = lax.ppermute(last, axis, up)  47.4 us
    ppermute x14, waiting for transfers between devices, extended(): after = lax.ppermute(first, axis, down)  45.6 us
    ppermute x14, starting transfers between devices, extended(): after = lax.ppermute(first, axis, down)  18.2 us
  transfers between devices with their start and end apart: 28, of which 20 were waited for; matrix products, arithmetic and copies ran while one was open for 0% of the time, Pallas kernels for 0%

commit v1 on v0

v1 whole, which is shorter than its diff:
```python
import functools

import jax
import jax.numpy as jnp
from jax import lax
from jax.experimental import pallas as pl
from jax.experimental.pallas import tpu as pltpu
from jax.sharding import PartitionSpec as P

DT_HJB = 0.5
NU_HJB = 0.25
COUPLE = 0.5
PENALTY = 2.0
DT_FP = 0.25
ABSORB = 4.0
SHIFT = 7.0

X0 = 4
Y0 = 8
MESH = pl.DeviceIdType.MESH


class Link:
    def __init__(self, src, dst, send, recv, device, can_send, can_recv):
        self.copy = pltpu.make_async_remote_copy(
            src_ref=src, dst_ref=dst, send_sem=send, recv_sem=recv,
            device_id=device, device_id_type=MESH)
        self.can_send, self.can_recv = can_send, can_recv

    def start(self):
        pl.when(self.can_send)(lambda: self.copy.start())

    def wait_recv(self):
        pl.when(self.can_recv)(lambda: self.copy.wait_recv())

    def wait_send(self):
        pl.when(self.can_send)(lambda: self.copy.wait_send())


def kernel(nbx, nby, t_in, m_in, p_in, h_in, v_out, s_out,
           T, C, D, M, V, G, B1, Q, D4, POT, HB, PKS, PKR, OUT, PA, PB,
           ssem, rsem, asend, arecv, bsend, brecv, lsem):
    nx, ny, nz = t_in.shape
    bx, by = lax.axis_index("bx"), lax.axis_index("by")
    XE, YE = nx + 2 * X0, ny + 2 * Y0
    X1, Y1 = X0 + nx, Y0 + ny
    barrier = pltpu.get_barrier_semaphore()
    for k in range(1, nby):
        pl.semaphore_signal(barrier, inc=1, device_id=(bx, lax.rem(by + k, nby)), device_id_type=MESH)
    for k in range(1, nbx):
        pl.semaphore_signal(barrier, inc=1, device_id=(lax.rem(bx + k, nbx), by), device_id_type=MESH)

    own = (pl.ds(X0, nx), pl.ds(Y0, ny))
    loads = [
        pltpu.make_async_copy(h_in, HB.at[1, 1], lsem.at[3]),
        pltpu.make_async_copy(m_in, D.at[own], lsem.at[1]),
        pltpu.make_async_copy(p_in, POT, lsem.at[2]),
        pltpu.make_async_copy(t_in, T.at[own], lsem.at[0]),
    ]
    for c in loads:
        c.start()

    has_xl, has_xu = bx > 0, bx < nbx - 1
    has_yl, has_yu = by > 0, by < nby - 1
    count = [0]

    def link(src, dst, device, can_send, can_recv):
        i = count[0]
        count[0] += 1
        return Link(src, dst, ssem.at[i], rsem.at[i], device, can_send, can_recv)

    def to_x_up(src, dst):
        return link(src, dst, (bx + 1, by), has_xu, has_xl)

    def to_x_down(src, dst):
        return link(src, dst, (bx - 1, by), has_xl, has_xu)

    def to_y_up(src, dst):
        return link(src, dst, (bx, by + 1), has_yu, has_yl)

    def to_y_down(src, dst):
        return link(src, dst, (bx, by - 1), has_yl, has_yu)

    def x_links(buf, w):
        rows = pl.ds(Y0, ny)
        return [to_x_up(buf.at[pl.ds(X1 - w, w), rows], buf.at[pl.ds(X0 - w, w), rows]),
                to_x_down(buf.at[pl.ds(X0, w), rows], buf.at[pl.ds(X1, w), rows])]

    def y_links(src, dst, planes):
        return [to_y_up(src.at[0, planes], dst.at[0, planes]),
                to_y_down(src.at[1, planes], dst.at[1, planes])]

    def y_links_field(buf, planes):
        return [to_y_up(buf.at[planes, pl.ds(Y1 - 8, 8)], buf.at[planes, pl.ds(0, 8)]),
                to_y_down(buf.at[planes, pl.ds(Y0, 8)], buf.at[planes, pl.ds(Y1, 8)])]

    def zero_planes(lo):
        for buf in (T, C, D, G):
            buf[pl.ds(lo, X0)] = jnp.zeros((X0, YE, nz), jnp.float32)

    pl.when(jnp.logical_not(has_xl))(lambda: zero_planes(0))
    pl.when(jnp.logical_not(has_xu))(lambda: zero_planes(X1))

    def column(block, x, rows, first):
        line = HB[block[0], block[1], pl.ds(x, 1), :].astype(jnp.float32)
        lanes = lax.broadcasted_iota(jnp.int32, (rows, ny), 1)
        subs = lax.broadcasted_iota(jnp.int32, (rows, ny), 0) + first
        return jnp.sum(jnp.where(lanes == subs, line, 0.0), axis=1, keepdims=True)

    def blocked(block, x, rows, first):
        level = lax.broadcasted_iota(jnp.int32, (rows, nz), 1).astype(jnp.float32)
        return jnp.where(level < column(block, x, rows, first), 1.0, 0.0)

    for c in loads[:3]:
        c.wait()

    @pl.loop(0, nx)
    def _(x):
        b = blocked((1, 1), x, ny, 0)
        D4[X0 + x, pl.ds(Y0, ny), :] = ABSORB * b
        C[X0 + x, pl.ds(Y0, ny), :] = POT[x] + COUPLE * D[X0 + x, pl.ds(Y0, ny), :] + PENALTY * b

    loads[3].wait()
    row8 = lax.broadcasted_iota(jnp.int32, (8, nz), 0)

    def pack(i, with_density):
        ys = pl.ds(Y1 - 8, 8)
        low = pltpu.roll(D[i, ys, :], 3, 0) if with_density else jnp.zeros((8, nz), jnp.float32)
        PKS[0, i] = jnp.where(row8 >= 5, T[i, ys, :], jnp.where(row8 >= 3, pltpu.roll(C[i, ys, :], 5, 0), low))
        ys = pl.ds(Y0, 8)
        high = pltpu.roll(D[i, ys, :], 5, 0) if with_density else jnp.zeros((8, nz), jnp.float32)
        PKS[1, i] = jnp.where(row8 < 3, T[i, ys, :], jnp.where(row8 < 5, pltpu.roll(C[i, ys, :], 3, 0), high))

    @pl.loop(X0, X1)
    def _(i):
        pack(i, True)

    pl.semaphore_wait(barrier, (nby - 1) + (nbx - 1))

    hx = [to_x_up(HB.at[1, 1], HB.at[0, 1]), to_x_down(HB.at[1, 1], HB.at[2, 1])]
    hy = [to_y_up(HB.at[1, 1], HB.at[1, 0]), to_y_down(HB.at[1, 1], HB.at[1, 2])]
    tx, cx, dx = x_links(T, 3), x_links(C, 2), x_links(D, 1)
    py = y_links(PKS, PKR, pl.ds(X0, nx))
    for c in hx + tx + cx + dx + hy + py:
        c.start()
    for c in hx + tx + cx:
        c.wait_recv()
    for i in (X0 - 2, X0 - 1, X1, X1 + 1):
        pack(i, False)
    pc = y_links(PKS, PKR, pl.ds(X0 - 2, 2)) + y_links(PKS, PKR, pl.ds(X1, 2))
    hc = []
    for side, has in ((0, has_xl), (2, has_xu)):
        up, down = has_yu & has, has_yl & has
        rup, rdown = has_yl & has, has_yu & has
        hc.append(link(HB.at[side, 1], HB.at[side, 0], (bx, by + 1), up, rup))
        hc.append(link(HB.at[side, 1], HB.at[side, 2], (bx, by - 1), down, rdown))
    for c in pc + hc:
        c.start()
    for c in dx + hy + py + pc + hc:
        c.wait_recv()

    keep_l = jnp.where(has_yl, 8, 0)
    keep_u = jnp.where(has_yu, 8, 0)

    @pl.loop(X0 - 2, X1 + 2)
    def _(i):
        got = jnp.where(row8 < keep_l, PKR[0, i], 0.0)
        T[i, pl.ds(0, 8), :] = got
        C[i, pl.ds(0, 8), :] = pltpu.roll(got, 3, 0)
        D[i, pl.ds(0, 8), :] = pltpu.roll(got, 5, 0)
        got = jnp.where(row8 < keep_u, PKR[1, i], 0.0)
        T[i, pl.ds(Y1, 8), :] = got
        C[i, pl.ds(Y1, 8), :] = pltpu.roll(got, 5, 0)
        D[i, pl.ds(Y1, 8), :] = pltpu.roll(got, 3, 0)

    rows = lax.broadcasted_iota(jnp.int32, (YE, nz), 0)
    lane = lax.broadcasted_iota(jnp.int32, (YE, nz), 1)
    first_row = jnp.where(has_yl, 0, Y0)
    last_row = jnp.where(has_yu, YE, Y1)
    first_plane = jnp.where(has_xl, 0, X0)
    last_plane = jnp.where(has_xu, XE, X1)

    def inside(i, v):
        end = jnp.where((i >= first_plane) & (i < last_plane), last_row, 0)
        return jnp.where((rows >= first_row) & (rows < end), v, 0.0)

    def sides(v):
        return (pltpu.roll(v, YE - 1, 0), pltpu.roll(v, 1, 0),
                jnp.where(lane == nz - 1, 0.0, pltpu.roll(v, nz - 1, 1)),
                jnp.where(lane == 0, 0.0, pltpu.roll(v, 1, 1)))

    def hjb(src, dst, lo, hi):
        @pl.loop(lo, hi)
        def _(i):
            v = src[i]
            yu, yl, zu, zl = sides(v)
            lap = -6.0 * v
            ham = jnp.zeros_like(v)
            for u, l in ((src[i + 1], src[i - 1]), (yu, yl), (zu, zl)):
                lap = lap + u + l
                ham = ham + jnp.square(jnp.maximum(v - l, 0.0)) + jnp.square(jnp.minimum(u - v, 0.0))
            dst[i] = inside(i, v + DT_HJB * (NU_HJB * lap - 0.5 * ham + C[i]))

    hjb(T, M, X0 - 2, X1 + 2)
    hjb(M, V, X0 - 1, X1 + 1)
    store_v = pltpu.make_async_copy(V.at[own], v_out, lsem.at[0])
    store_v.start()

    mid = slice(Y0, Y1)

    @pl.loop(X0, X1)
    def _(i):
        v, m = V[i], D[i]
        vs, ms = sides(v), sides(m)
        vx = [V[i + 1, pl.ds(Y0, ny), :], V[i - 1, pl.ds(Y0, ny), :]]
        mx = [D[i + 1, pl.ds(Y0, ny), :], D[i - 1, pl.ds(Y0, ny), :]]
        vs = vx + [a[mid] for a in vs]
        ms = mx + [a[mid] for a in ms]
        v, m = v[mid], m[mid]
        div = jnp.zeros_like(m)
        for a in (0, 2, 4):
            s = v - vs[a]
            t = vs[a + 1] - v
            div = div + (jnp.maximum(s, 0.0) * m + jnp.minimum(s, 0.0) * ms[a]
                         - jnp.maximum(t, 0.0) * ms[a + 1] - jnp.minimum(t, 0.0) * m)
        G[i, pl.ds(Y0, ny), :] = m - DT_FP * div

    gx = x_links(G, 4)
    gy = y_links_field(G, pl.ds(X0, nx))
    for c in gx + gy:
        c.start()

    @pl.loop(0, nx)
    def _(x):
        D4[X0 + x, pl.ds(0, 8), :] = ABSORB * blocked((1, 0), x, 8, ny - 8)
        D4[X0 + x, pl.ds(Y1, 8), :] = ABSORB * blocked((1, 2), x, 8, 0)

    def halo_obstacles(side, x, i):
        D4[i, pl.ds(0, 8), :] = ABSORB * blocked((side, 0), x, 8, ny - 8)
        D4[i, pl.ds(Y0, ny), :] = ABSORB * blocked((side, 1), x, ny, 0)
        D4[i, pl.ds(Y1, 8), :] = ABSORB * blocked((side, 2), x, 8, 0)

    @pl.loop(0, 3)
    def _(j):
        halo_obstacles(0, nx - 3 + j, X0 - 3 + j)
        halo_obstacles(2, j, X1 + j)

    for c in gx:
        c.wait_recv()
    gc = y_links_field(G, pl.ds(1, 3)) + y_links_field(G, pl.ds(X1, 3))
    for c in gc:
        c.start()
    for c in gy + gc:
        c.wait_recv()

    def zero_rows(lo):
        G[:, pl.ds(lo, 8), :] = jnp.zeros((XE, 8, nz), jnp.float32)

    pl.when(jnp.logical_not(has_yl))(lambda: zero_rows(0))
    pl.when(jnp.logical_not(has_yu))(lambda: zero_rows(Y1))

    def shifted(src, i):
        v = src[i]
        yu, yl, zu, zl = sides(v)
        return v, D4[i] * v - (src[i + 1] + src[i - 1] + (yu + yl) + (zu + zl))

    R = M

    @pl.loop(X0 - 3, X1 + 3)
    def _(i):
        v, b = shifted(G, i)
        R[i] = inside(i, (1.0 - SHIFT) * v - b)

    @pl.loop(X0 - 2, X1 + 2)
    def _(i):
        B1[i] = inside(i, shifted(R, i)[1])

    @pl.loop(X0 - 1, X1 + 1)
    def _(i):
        Q[i] = inside(i, shifted(B1, i)[1])

    def moments(i, sums):
        ys = pl.ds(Y0, ny)
        r, b = R[i, ys, :], B1[i, ys, :]
        full = Q[i]
        yu = pltpu.roll(full, YE - 1, 0)[mid]
        zu = jnp.where(lane == nz - 1, 0.0, pltpu.roll(full, nz - 1, 1))[mid]
        q = full[mid]
        image = D4[i, ys, :] * q - 2.0 * (Q[i + 1, ys, :] + yu + zu)
        terms = (r * r, r * b, b * b, b * q, q * q, q * image)

        def fold(a):
            a = a.reshape(ny // 8, 8, nz).sum(axis=0)
            return sum(a[:, j:j + 128] for j in range(0, nz, 128))

        return tuple(s + fold(a) for s, a in zip(sums, terms))

    zero = jnp.zeros((8, 128), jnp.float32)
    sums = lax.fori_loop(X0, X1, moments, (zero,) * 6)
    tile_row = lax.broadcasted_iota(jnp.int32, (8, 128), 0)
    tile = zero
    for k, s in enumerate(sums):
        tile = jnp.where(tile_row == k, jnp.sum(s, axis=0, keepdims=True), tile)

    def all_sum(slots, value, n, me, device, send, recv):
        slots[me] = value
        copies = []
        for k in range(1, n):
            c = pltpu.make_async_remote_copy(
                src_ref=slots.at[me], dst_ref=slots.at[me], send_sem=send.at[k - 1], recv_sem=recv.at[k - 1],
                device_id=device(lax.rem(me + k, n)), device_id_type=MESH)
            c.start()
            copies.append(c)
        for k in range(1, n):
            source = lax.rem(me + n - k, n)
            pltpu.make_async_remote_copy(
                src_ref=slots.at[source], dst_ref=slots.at[source], send_sem=send.at[k - 1], recv_sem=recv.at[k - 1],
                device_id=device(source), device_id_type=MESH).wait_recv()
        return copies, jnp.sum(slots[...], axis=0)

    ca, tile = all_sum(PA, tile, nby, by, lambda j: (bx, j), asend, arecv)
    cb, tile = all_sum(PB, tile, nbx, bx, lambda j: (j, by), bsend, brecv)
    tile = jnp.broadcast_to(jnp.sum(tile, axis=1, keepdims=True), (8, 128))
    nu = [tile[k:k + 1] for k in range(6)]

    def dot(p, q, s):
        total = 0.0
        for i, a in enumerate(p):
            for j, b in enumerate(q):
                total = total + a * b * nu[i + j + s]
        return total

    def energy(p):
        return SHIFT * dot(p, p, 0) + dot(p, p, 1)

    def step_of(rr, p):
        return jnp.clip(rr / energy(p), 1.0 / 17.0, 1.0)

    one = jnp.ones_like(nu[0])
    rr = nu[0]
    p, r = (one,), (one,)
    x = None
    for it in range(3):
        a = step_of(rr, p)
        x = [a * c for c in p] if x is None else [x[j] + a * p[j] if j < len(x) else a * p[j] for j in range(len(p))]
        if it == 2:
            break
        image = [SHIFT * c for c in p] + [jnp.zeros_like(one)]
        for j, c in enumerate(p):
            image[j + 1] = image[j + 1] + c
        r = tuple((r[j] if j < len(r) else 0.0) - a * image[j] for j in range(len(image)))
        new = jnp.maximum(dot(r, r, 0), 0.0)
        beta = new / rr
        p = tuple(r[j] + (beta * p[j] if j < len(p) else 0.0) for j in range(len(r)))
        rr = new
    x = [jnp.concatenate([c] * (nz // 128), axis=1) for c in x]

    @pl.loop(X0, X1)
    def _(i):
        ys = pl.ds(Y0, ny)
        OUT[i - X0] = G[i, ys, :] + x[0] * R[i, ys, :] + x[1] * B1[i, ys, :] + x[2] * Q[i, ys, :]

    store_s = pltpu.make_async_copy(OUT, s_out, lsem.at[1])
    store_s.start()
    for c in hx + tx + cx + dx + hy + py + pc + hc + gx + gy + gc:
        c.wait_send()
    for c in ca + cb:
        c.wait_send()
    store_v.wait()
    store_s.wait()


LINKS = 32


def per_device(nbx, nby, t, m, p, h):
    nx, ny, nz = t.shape
    ext = pltpu.VMEM((nx + 2 * X0, ny + 2 * Y0, nz), jnp.float32)
    packed = pltpu.VMEM((2, nx + 2 * X0, 8, nz), jnp.float32)
    block = pltpu.VMEM((nx, ny, nz), jnp.float32)
    any_spec = pl.BlockSpec(memory_space=pl.ANY)
    out = jax.ShapeDtypeStruct(t.shape, jnp.float32)
    return pl.pallas_call(
        functools.partial(kernel, nbx, nby),
        out_shape=(out, out),
        in_specs=[any_spec] * 4,
        out_specs=(any_spec, any_spec),
        scratch_shapes=[ext] * 9 + [
            block, pltpu.VMEM((3, 3, nx, ny), jnp.int32), packed, packed, block,
            pltpu.VMEM((nby, 8, 128), jnp.float32), pltpu.VMEM((nbx, 8, 128), jnp.float32),
            pltpu.SemaphoreType.DMA((LINKS,)), pltpu.SemaphoreType.DMA((LINKS,)),
            pltpu.SemaphoreType.DMA((nby - 1,)), pltpu.SemaphoreType.DMA((nby - 1,)),
            pltpu.SemaphoreType.DMA((nbx - 1,)), pltpu.SemaphoreType.DMA((nbx - 1,)),
            pltpu.SemaphoreType.DMA((4,)),
        ],
        compiler_params=pltpu.CompilerParams(
            collective_id=0, has_side_effects=True, vmem_limit_bytes=32 * 1024 * 1024),
        name="mean_field_step",
    )(t, m, p, h)


def solution(mesh):
    cells, plane = P("bx", "by", None), P("bx", "by")
    return jax.shard_map(
        functools.partial(per_device, mesh.shape["bx"], mesh.shape["by"]),
        mesh=mesh, in_specs=(cells, cells, cells, plane), out_specs=(cells, cells), check_vma=False)
```

time: 340 us -> 46.1 us (0.14)
  blocking collectives: 206 us -> 0 us
  starting transfers between devices: 65.6 us -> 0 us
  waiting for transfers between devices: 47.9 us -> 0 us
  Pallas kernels: 0 us -> 40.3 us
  other arithmetic: 9.39 us -> 0 us
  between operations: 7.67 us -> 0.65 us
    psum x5 -> x0, blocking collectives: 206 us -> none  [the longest x3 121 us: residual_squares(): return lax.psum(jnp.sum(residual * residual), ('bx', 'by'))]
    ppermute x28 -> x0, starting transfers between devices: 65.6 us -> none  [the longest x14 47.4 us: extended(): before = lax.ppermute(last, axis, up)]
    ppermute x28 -> x0, waiting for transfers between devices: 47.9 us -> none  [the longest x14 45.6 us: extended(): after = lax.ppermute(first, axis, down)]
    pallas_call x0 -> x1, Pallas kernels: none -> 40.3 us  [per_device(): pl.pallas_call(functools.partial(kernel, nbx, nby), out_shape=(out, out),...]
    reduce_sum x5 -> x0, other arithmetic: 4.14 us -> none  [the longest x3 2.72 us: per_device(): alpha = norm_now / lax.psum(jnp.sum(direction * image), ('bx', 'by'))]
    unnamed x12 -> x10, local copies, waits for them, and re-layouts: 1 us -> 4.95 us
  transfers between devices with their start and end apart: 28 -> 0, of which waited for: 20 -> 0; matrix products, arithmetic and copies ran while one was open for 0% -> 0% of each run, Pallas kernels for 0% -> 0%
where the time goes in v1:
time: 46.1 us; the launch traced here: 45.9 us
  Pallas kernels  40.3 us (87%)
  local copies, waits for them, and re-layouts  4.95 us (11%)
  between operations  0.65 us (1%)
    pallas_call x1, Pallas kernels, per_device(): pl.pallas_call(functools.partial(kernel, nbx, nby), out_shape=(out, out),...  40.3 us
    unnamed x10, local copies, waits for them, and re-layouts  4.95 us

profile of v1, /device:TPU:0, one launch (start us, length us, event | category | flops | bytes accessed | tf_op | source)
XLA Modules:
  0.0 45.9 jit_solution(14811006564442532975)
XLA Ops:
  0.6 0.0 copy-start
  0.6 0.9 %copy-done = f32[16,16,256]{2,1,0:T(8,128)S(1)} copy-done((f32[16,16,256]{2,1,0:T(8,128)S(1)}, f32[16,16,256]{2,1,0:T(8,128)}, u32[]{:S(2)}) %copy-start) | copy-done | bytes 262168
  1.6 0.0 copy-start.1
  1.6 0.9 %copy-done.1 = f32[16,16,256]{2,1,0:T(8,128)S(1)} copy-done((f32[16,16,256]{2,1,0:T(8,128)S(1)}, f32[16,16,256]{2,1,0:T(8,128)}, u32[]{:S(2)}) %copy-start.1) | copy-done | bytes 262168
  2.5 0.0 copy-start.2
  2.5 0.9 %copy-done.2 = f32[16,16,256]{2,1,0:T(8,128)S(1)} copy-done((f32[16,16,256]{2,1,0:T(8,128)S(1)}, f32[16,16,256]{2,1,0:T(8,128)}, u32[]{:S(2)}) %copy-start.2) | copy-done | bytes 262168
  3.5 0.0 copy-start.3
  3.5 0.7 %copy-done.3 = s32[16,16]{1,0:T(8,128)S(1)} copy-done((s32[16,16]{1,0:T(8,128)S(1)}, s32[16,16]{1,0:T(8,128)}, u32[]{:S(2)}) %copy-start.3) | copy-done | bytes 1048
  4.2 40.3 %mean_field_step.1 = (f32[16,16,256]{2,1,0:T(8,128)S(1)}, f32[16,16,256]{2,1,0:T(8,128)S(1)}) custom-call(f32[16,16,256]{2,1,0:T(8,128)S(1)} %copy-done, f32[16,16,256]{2,1,0:T(8,128)S(1)} %copy-done.1, f32[16,16,256]{2,1,0:T(8,128)S(1)} %copy-done.2, s32[16,16]{1,0:T(8,128)S(1)} %copy-done.3), custom_call_target="tpu_custom_call" | custom-call | tf_op jit(solution)/shard_map/mean_field_step/pallas_call | solution.py:383
  44.5 0.7 %copy.8 = f32[16,16,256]{2,1,0:T(8,128)} copy(f32[16,16,256]{2,1,0:T(8,128)S(1)} %get-tuple-element.4) | data formatting | bytes 524288
  45.2 0.7 %copy.9 = f32[16,16,256]{2,1,0:T(8,128)} copy(f32[16,16,256]{2,1,0:T(8,128)S(1)} %get-tuple-element.5) | data formatting | bytes 524288
Async XLA Ops:
  0.6 1.0 %copy-start = (f32[16,16,256]{2,1,0:T(8,128)S(1)}, f32[16,16,256]{2,1,0:T(8,128)}, u32[]{:S(2)}) copy-start(f32[16,16,256]{2,1,0:T(8,128)} %t_in.1) | copy-start | bytes 786436
  1.6 0.9 %copy-start.1 = (f32[16,16,256]{2,1,0:T(8,128)S(1)}, f32[16,16,256]{2,1,0:T(8,128)}, u32[]{:S(2)}) copy-start(f32[16,16,256]{2,1,0:T(8,128)} %m_in.1) | copy-start | bytes 786436
  2.5 0.9 %copy-start.2 = (f32[16,16,256]{2,1,0:T(8,128)S(1)}, f32[16,16,256]{2,1,0:T(8,128)}, u32[]{:S(2)}) copy-start(f32[16,16,256]{2,1,0:T(8,128)} %p_in.1) | copy-start | bytes 786436
  3.5 0.7 %copy-start.3 = (s32[16,16]{1,0:T(8,128)S(1)}, s32[16,16]{1,0:T(8,128)}, u32[]{:S(2)}) copy-start(s32[16,16]{1,0:T(8,128)} %h_in.1) | copy-start | bytes 3076

commit v2 on v1

v2 whole, which is shorter than its diff:
```python
import functools

import jax
import jax.numpy as jnp
from jax import lax
from jax.experimental import pallas as pl
from jax.experimental.pallas import tpu as pltpu
from jax.sharding import PartitionSpec as P

DT_HJB = 0.5
NU_HJB = 0.25
COUPLE = 0.5
PENALTY = 2.0
DT_FP = 0.25
ABSORB = 4.0
SHIFT = 7.0

X0 = 4
HALO = 8
MESH = pl.DeviceIdType.MESH


class Link:
    def __init__(self, src, dst, send, recv, device, can_send, can_recv):
        self.copy = pltpu.make_async_remote_copy(
            src_ref=src, dst_ref=dst, send_sem=send, recv_sem=recv,
            device_id=device, device_id_type=MESH)
        self.can_send, self.can_recv = can_send, can_recv

    def start(self):
        pl.when(self.can_send)(lambda: self.copy.start())

    def wait_recv(self):
        pl.when(self.can_recv)(lambda: self.copy.wait_recv())

    def wait_send(self):
        pl.when(self.can_send)(lambda: self.copy.wait_send())


def kernel(nbx, nby, t_in, m_in, p_in, h_in, v_out, s_out,
           T, C, D, M, V, G, B1, Q, D4, POT, HB, PKS, PKR, GR, PA, PB,
           ssem, rsem, asend, arecv, bsend, brecv, lsem):
    nx, ny, nz = POT.shape
    bx, by = lax.axis_index("bx"), lax.axis_index("by")
    XE, YE, X1 = nx + 2 * X0, ny + HALO, X0 + nx
    barrier = pltpu.get_barrier_semaphore()
    for k in range(1, nby):
        pl.semaphore_signal(barrier, inc=1, device_id=(bx, lax.rem(by + k, nby)), device_id_type=MESH)
    for k in range(1, nbx):
        pl.semaphore_signal(barrier, inc=1, device_id=(lax.rem(bx + k, nbx), by), device_id_type=MESH)

    rows = pl.ds(0, ny)
    beyond = pl.ds(ny, HALO)
    loads = [
        pltpu.make_async_copy(h_in, HB.at[1, 1], lsem.at[3]),
        pltpu.make_async_copy(m_in, D.at[pl.ds(X0, nx), rows], lsem.at[1]),
        pltpu.make_async_copy(p_in, POT, lsem.at[2]),
        pltpu.make_async_copy(t_in, T.at[pl.ds(X0, nx), rows], lsem.at[0]),
    ]
    for c in loads:
        c.start()

    has_xl, has_xu = bx > 0, bx < nbx - 1
    has_yl, has_yu = by > 0, by < nby - 1
    count = [0]

    def link(src, dst, device, can_send, can_recv):
        i = count[0]
        count[0] += 1
        return Link(src, dst, ssem.at[i], rsem.at[i], device, can_send, can_recv)

    def x_up(src, dst):
        return link(src, dst, (bx + 1, by), has_xu, has_xl)

    def x_down(src, dst):
        return link(src, dst, (bx - 1, by), has_xl, has_xu)

    def y_up(src, dst, has=True):
        return link(src, dst, (bx, by + 1), has_yu & has, has_yl & has)

    def y_down(src, dst, has=True):
        return link(src, dst, (bx, by - 1), has_yl & has, has_yu & has)

    def x_links(buf, w):
        return [x_up(buf.at[pl.ds(X1 - w, w), rows], buf.at[pl.ds(X0 - w, w), rows]),
                x_down(buf.at[pl.ds(X0, w), rows], buf.at[pl.ds(X1, w), rows])]

    def packed_links(planes):
        return [y_up(PKS.at[0, planes], PKR.at[0, planes]), y_down(PKS.at[1, planes], PKR.at[1, planes])]

    def field_links(planes):
        return [y_up(G.at[planes, pl.ds(ny - 8, 8)], GR.at[0, planes]),
                y_down(G.at[planes, pl.ds(0, 8)], GR.at[1, planes])]

    def zero_planes(lo):
        for buf in (T, C, D, M, V, G, B1, Q):
            buf[pl.ds(lo, X0)] = jnp.zeros((X0, YE, nz), jnp.float32)

    pl.when(jnp.logical_not(has_xl))(lambda: zero_planes(0))
    pl.when(jnp.logical_not(has_xu))(lambda: zero_planes(X1))

    def below(k):
        return jnp.where(has_xl, X0 - k, X0)

    def above(k):
        return jnp.where(has_xu, X1 + k, X1)

    def column(side, part, x, n, first):
        line = HB[side, part, pl.ds(x, 1), :].astype(jnp.float32)
        lanes = lax.broadcasted_iota(jnp.int32, (n, ny), 1)
        subs = lax.broadcasted_iota(jnp.int32, (n, ny), 0) + first
        return jnp.sum(jnp.where(lanes == subs, line, 0.0), axis=1, keepdims=True)

    def level_mask(col, high):
        level = lax.broadcasted_iota(jnp.int32, (col.shape[0], nz), 1).astype(jnp.float32)
        return jnp.where(level < col, high, 0.0)

    for c in loads[:3]:
        c.wait()

    @pl.loop(0, nx)
    def _(x):
        b = level_mask(column(1, 1, x, ny, 0), ABSORB)
        D4[X0 + x, rows, :] = b
        C[X0 + x, rows, :] = POT[x] + COUPLE * D[X0 + x, rows, :] + (PENALTY / ABSORB) * b

    loads[3].wait()
    row8 = lax.broadcasted_iota(jnp.int32, (8, nz), 0)

    def pack(i, with_density):
        ys = pl.ds(ny - 8, 8)
        low = pltpu.roll(D[i, ys, :], 3, 0) if with_density else jnp.zeros((8, nz), jnp.float32)
        PKS[0, i] = jnp.where(row8 >= 5, T[i, ys, :], jnp.where(row8 >= 3, pltpu.roll(C[i, ys, :], 5, 0), low))
        ys = pl.ds(0, 8)
        high = pltpu.roll(D[i, ys, :], 5, 0) if with_density else jnp.zeros((8, nz), jnp.float32)
        PKS[1, i] = jnp.where(row8 < 3, T[i, ys, :], jnp.where(row8 < 5, pltpu.roll(C[i, ys, :], 3, 0), high))

    @pl.loop(X0, X1)
    def _(i):
        pack(i, True)

    pl.semaphore_wait(barrier, (nby - 1) + (nbx - 1))

    hx = [x_up(HB.at[1, 1], HB.at[0, 1]), x_down(HB.at[1, 1], HB.at[2, 1])]
    hy = [y_up(HB.at[1, 1], HB.at[1, 0]), y_down(HB.at[1, 1], HB.at[1, 2])]
    py = packed_links(pl.ds(X0, nx))
    tx, cx, dx = x_links(T, 3), x_links(C, 2), x_links(D, 1)
    for c in hx + hy + tx + py + cx + dx:
        c.start()

    keep = (row8 >= jnp.where(has_yu, 0, 4)) & (row8 < jnp.where(has_yl, 8, 4))
    upper = row8 < 4

    def join(a, b):
        return jnp.where(keep, jnp.where(upper, b, a), 0.0)

    def unpack(i):
        a, b = PKR[0, i], PKR[1, i]
        T[i, beyond, :] = join(a, b)
        C[i, beyond, :] = join(pltpu.roll(a, 3, 0), pltpu.roll(b, 5, 0))
        D[i, beyond, :] = join(pltpu.roll(a, 5, 0), pltpu.roll(b, 3, 0))

    def loop(lo, hi, f):
        @pl.loop(lo, hi)
        def _(i):
            f(i)

    lane = lax.broadcasted_iota(jnp.int32, (YE, 128), 1)

    def z_up(v):
        n = v.shape[0]
        tiles = [pltpu.roll(v[:, j:j + 128], 127, 1) for j in range(0, nz, 128)]
        tiles.append(jnp.zeros_like(tiles[0]))
        return jnp.concatenate([jnp.where(lane[:n] == 127, b, a) for a, b in zip(tiles, tiles[1:])], axis=1)

    def z_low(v, edge=None):
        n = v.shape[0]
        tiles = [jnp.zeros((n, 128), jnp.float32) if edge is None else edge]
        tiles += [pltpu.roll(v[:, j:j + 128], 1, 1) for j in range(0, nz, 128)]
        return jnp.concatenate([jnp.where(lane[:n] == 0, a, b) for a, b in zip(tiles, tiles[1:])], axis=1)

    def put(dst, i, v):
        dst[i, rows, :] = v[:ny]
        dst[i, beyond, :] = jnp.where(keep, v[ny:], 0.0)

    def hjb(src, dst, lo, hi, out=None):
        def f(i):
            v = src[i]
            lap = -6.0 * v
            ham = jnp.zeros_like(v)
            for u, l in ((src[i + 1], src[i - 1]), (pltpu.roll(v, YE - 1, 0), pltpu.roll(v, 1, 0)),
                         (z_up(v), z_low(v))):
                lap = lap + (u + l)
                ham = ham + jnp.square(jnp.maximum(v - l, 0.0)) + jnp.square(jnp.minimum(u - v, 0.0))
            new = v + DT_HJB * (NU_HJB * lap - 0.5 * ham + C[i])
            put(dst, i, new)
            if out is not None:
                out[i - X0] = new[:ny]
        loop(lo, hi, f)

    def flux(v, vu, m, mu):
        s = v - vu
        return jnp.maximum(s, 0.0) * m + jnp.minimum(s, 0.0) * mu

    def x_flux(i):
        return flux(V[i, rows, :], V[i + 1, rows, :], D[i, rows, :], D[i + 1, rows, :])

    def transport(lo, hi):
        def f(i, before):
            v, m = V[i], D[i]
            fy = flux(v, pltpu.roll(v, YE - 1, 0), m, pltpu.roll(m, YE - 1, 0))
            ly = pltpu.roll(fy, 1, 0)[:ny]
            v, m = v[:ny], m[:ny]
            fz = flux(v, z_up(v), m, z_up(m))
            lz = z_low(fz, jnp.minimum(-v[:, :128], 0.0) * m[:, :128])
            fx = x_flux(i)
            G[i, rows, :] = m - DT_FP * ((fx - before) + (fy[:ny] - ly) + (fz - lz))
            return fx
        lax.fori_loop(lo, hi, f, x_flux(lo - 1))

    def beyond_obstacles(side, x, i):
        col = jnp.where(lax.broadcasted_iota(jnp.int32, (8, 1), 0) < 4,
                        column(side, 2, x, 8, 0), column(side, 0, x, 8, ny - 8))
        D4[i, beyond, :] = level_mask(col, ABSORB)

    for c in hy + py:
        c.wait_recv()
    loop(X0, X1, unpack)
    hjb(T, M, X0 + 1, X1 - 1)
    hjb(M, V, X0 + 2, X1 - 2, v_out)
    transport(X0 + 3, X1 - 3)
    loop(0, nx, lambda x: beyond_obstacles(1, x, X0 + x))

    for c in hx + tx + cx:
        c.wait_recv()
    corners = ((0, has_xl, X0 - 2), (2, has_xu, X1))
    pc = []
    for side, has, lo in corners:
        loop(lo, lo + 2, lambda i: pack(i, False))
        pc += packed_links(pl.ds(lo, 2))
        pc.append(y_up(HB.at[side, 1], HB.at[side, 0], has))
        pc.append(y_down(HB.at[side, 1], HB.at[side, 2], has))
    for c in pc:
        c.start()
    for c in dx + pc:
        c.wait_recv()
    for side, has, lo in corners:
        loop(lo, lo + 2, unpack)
    hjb(T, M, below(2), X0 + 1)
    hjb(T, M, X1 - 1, above(2))
    hjb(M, V, below(1), X0)
    hjb(M, V, X1, above(1))
    hjb(M, V, X0, X0 + 2, v_out)
    hjb(M, V, X1 - 2, X1, v_out)
    transport(X0, X0 + 3)
    transport(X1 - 3, X1)

    gx = x_links(G, 4)
    gy = field_links(pl.ds(X0, nx))
    for c in gx + gy:
        c.start()

    def halo_obstacles(side, x, i):
        D4[i, rows, :] = level_mask(column(side, 1, x, ny, 0), ABSORB)
        beyond_obstacles(side, x, i)

    @pl.loop(0, 3)
    def _(j):
        halo_obstacles(0, nx - 3 + j, X0 - 3 + j)
        halo_obstacles(2, j, X1 + j)

    def merge(i):
        G[i, beyond, :] = join(GR[0, i], GR[1, i])

    def shifted(src, i):
        v = src[i]
        return v, D4[i] * v - ((src[i + 1] + src[i - 1]) + (pltpu.roll(v, YE - 1, 0) + pltpu.roll(v, 1, 0))
                               + (z_up(v) + z_low(v)))

    R = M

    def first(lo, hi):
        def f(i):
            v, b = shifted(G, i)
            put(R, i, (1.0 - SHIFT) * v - b)
        loop(lo, hi, f)

    def power(src, dst, lo, hi):
        loop(lo, hi, lambda i: put(dst, i, shifted(src, i)[1]))

    for c in gy:
        c.wait_recv()
    loop(X0, X1, merge)
    first(X0 + 1, X1 - 1)
    power(R, B1, X0 + 2, X1 - 2)
    power(B1, Q, X0 + 3, X1 - 3)

    for c in gx:
        c.wait_recv()
    gc = field_links(pl.ds(1, 3)) + field_links(pl.ds(X1, 3))
    for c in gc:
        c.start()
    for c in gc:
        c.wait_recv()
    loop(1, X0, merge)
    loop(X1, X1 + 3, merge)
    first(below(3), X0 + 1)
    first(X1 - 1, above(3))
    power(R, B1, below(2), X0 + 2)
    power(R, B1, X1 - 2, above(2))
    power(B1, Q, X0, X0 + 3)
    power(B1, Q, X1 - 3, above(1))

    def moments(i, sums):
        r, b = R[i, rows, :], B1[i, rows, :]
        full = Q[i]
        yu = pltpu.roll(full, YE - 1, 0)[:ny]
        q = full[:ny]
        image = D4[i, rows, :] * q - 2.0 * (Q[i + 1, rows, :] + yu + z_up(q))
        terms = (r * r, r * b, b * b, b * q, q * q, q * image)

        def fold(a):
            a = a.reshape(ny // 8, 8, nz).sum(axis=0)
            return sum(a[:, j:j + 128] for j in range(0, nz, 128))

        return tuple(s + fold(a) for s, a in zip(sums, terms))

    zero = jnp.zeros((8, 128), jnp.float32)
    sums = lax.fori_loop(X0, X1, moments, (zero,) * 6)
    tile_row = lax.broadcasted_iota(jnp.int32, (8, 128), 0)
    tile = zero
    for k, s in enumerate(sums):
        tile = jnp.where(tile_row == k, jnp.sum(s, axis=0, keepdims=True), tile)

    def all_sum(slots, value, n, me, device, send, recv):
        slots[me] = value
        copies = []
        for k in range(1, n):
            c = pltpu.make_async_remote_copy(
                src_ref=slots.at[me], dst_ref=slots.at[me], send_sem=send.at[k - 1], recv_sem=recv.at[k - 1],
                device_id=device(lax.rem(me + k, n)), device_id_type=MESH)
            c.start()
            copies.append(c)
        for k in range(1, n):
            source = lax.rem(me + n - k, n)
            pltpu.make_async_remote_copy(
                src_ref=slots.at[source], dst_ref=slots.at[source], send_sem=send.at[k - 1], recv_sem=recv.at[k - 1],
                device_id=device(source), device_id_type=MESH).wait_recv()
        return copies, jnp.sum(slots[...], axis=0)

    ca, tile = all_sum(PA, tile, nby, by, lambda j: (bx, j), asend, arecv)
    cb, tile = all_sum(PB, tile, nbx, bx, lambda j: (j, by), bsend, brecv)
    tile = jnp.broadcast_to(jnp.sum(tile, axis=1, keepdims=True), (8, 128))
    nu = [tile[k:k + 1] for k in range(6)]

    def dot(p, q, s):
        total = 0.0
        for i, a in enumerate(p):
            for j, b in enumerate(q):
                total = total + a * b * nu[i + j + s]
        return total

    def energy(p):
        return SHIFT * dot(p, p, 0) + dot(p, p, 1)

    def step_of(rr, p):
        return jnp.clip(rr / energy(p), 1.0 / 17.0, 1.0)

    one = jnp.ones_like(nu[0])
    rr = nu[0]
    p, r = (one,), (one,)
    x = None
    for it in range(3):
        a = step_of(rr, p)
        x = [a * c for c in p] if x is None else [x[j] + a * p[j] if j < len(x) else a * p[j] for j in range(len(p))]
        if it == 2:
            break
        image = [SHIFT * c for c in p] + [jnp.zeros_like(one)]
        for j, c in enumerate(p):
            image[j + 1] = image[j + 1] + c
        r = tuple((r[j] if j < len(r) else 0.0) - a * image[j] for j in range(len(image)))
        new = jnp.maximum(dot(r, r, 0), 0.0)
        beta = new / rr
        p = tuple(r[j] + (beta * p[j] if j < len(p) else 0.0) for j in range(len(r)))
        rr = new
    x = [jnp.concatenate([c] * (nz // 128), axis=1) for c in x]

    @pl.loop(X0, X1)
    def _(i):
        s_out[i - X0] = G[i, rows, :] + x[0] * R[i, rows, :] + x[1] * B1[i, rows, :] + x[2] * Q[i, rows, :]

    for c in hx + hy + tx + py + cx + dx + pc + gx + gy + gc:
        c.wait_send()
    for c in ca + cb:
        c.wait_send()


LINKS = 32


def per_device(nbx, nby, t, m, p, h):
    nx, ny, nz = t.shape
    ext = pltpu.VMEM((nx + 2 * X0, ny + HALO, nz), jnp.float32)
    packed = pltpu.VMEM((2, nx + 2 * X0, 8, nz), jnp.float32)
    out = jax.ShapeDtypeStruct(t.shape, jnp.float32)
    return pl.pallas_call(
        functools.partial(kernel, nbx, nby),
        out_shape=(out, out),
        in_specs=[pl.BlockSpec(memory_space=pl.ANY)] * 4,
        out_specs=(pl.BlockSpec(memory_space=pltpu.VMEM),) * 2,
        scratch_shapes=[ext] * 9 + [
            pltpu.VMEM((nx, ny, nz), jnp.float32), pltpu.VMEM((3, 3, nx, ny), jnp.int32), packed, packed, packed,
            pltpu.VMEM((nby, 8, 128), jnp.float32), pltpu.VMEM((nbx, 8, 128), jnp.float32),
            pltpu.SemaphoreType.DMA((LINKS,)), pltpu.SemaphoreType.DMA((LINKS,)),
            pltpu.SemaphoreType.DMA((nby - 1,)), pltpu.SemaphoreType.DMA((nby - 1,)),
            pltpu.SemaphoreType.DMA((nbx - 1,)), pltpu.SemaphoreType.DMA((nbx - 1,)),
            pltpu.SemaphoreType.DMA((4,)),
        ],
        compiler_params=pltpu.CompilerParams(collective_id=0, has_side_effects=True),
        name="mean_field_step",
    )(t, m, p, h)


def solution(mesh):
    cells, plane = P("bx", "by", None), P("bx", "by")
    return jax.shard_map(
        functools.partial(per_device, mesh.shape["bx"], mesh.shape["by"]),
        mesh=mesh, in_specs=(cells, cells, cells, plane), out_specs=(cells, cells), check_vma=False)
```

time: 46.1 us -> 44.4 us (0.963)
  local copies, waits for them, and re-layouts: 4.95 us -> 2.42 us
  Pallas kernels: 40.3 us -> 41.1 us
    unnamed x10 -> x4, local copies, waits for them, and re-layouts: 4.95 us -> 2.42 us
    pallas_call x1, Pallas kernels: 40.3 us -> 41.1 us  [per_device(): pl.pallas_call(functools.partial(kernel, nbx, nby), out_shape=(out, out),...]
where the time goes in v2:
time: 44.4 us; the launch traced here: 44.2 us
  Pallas kernels  41.1 us (93%)
  local copies, waits for them, and re-layouts  2.42 us (5%)
  between operations  0.65 us (1%)
    pallas_call x1, Pallas kernels, per_device(): pl.pallas_call(functools.partial(kernel, nbx, nby), out_shape=(out, out),...  41.1 us
    unnamed x4, local copies, waits for them, and re-layouts  2.42 us

profile of v2, /device:TPU:0, one launch (start us, length us, event | category | flops | bytes accessed | tf_op | source)
XLA Modules:
  0.0 44.2 jit_solution(8684662371125248395)
XLA Ops:
  0.6 41.1 %mean_field_step.1 = (f32[16,16,256]{2,1,0:T(8,128)}, f32[16,16,256]{2,1,0:T(8,128)}) custom-call(f32[16,16,256]{2,1,0:T(8,128)} %t_in.1, f32[16,16,256]{2,1,0:T(8,128)} %m_in.1, f32[16,16,256]{2,1,0:T(8,128)} %p_in.1, s32[16,16]{1,0:T(8,128)} %h_in.1), custom_call_target="tpu_custom_call" | custom-call | tf_op jit(solution)/shard_map/mean_field_step/pallas_call | solution.py:406
  41.8 0.0 copy-start
  41.8 1.7 %copy.8 = f32[16,16,256]{2,1,0:T(8,128)} copy(f32[16,16,256]{2,1,0:T(8,128)} %get-tuple-element.4) | data formatting | bytes 524288
  43.5 0.0 copy-done
  43.5 0.7 %copy.9 = f32[16,16,256]{2,1,0:T(8,128)} copy(f32[16,16,256]{2,1,0:T(8,128)S(1)} %copy-done) | data formatting | bytes 524288
Async XLA Ops:
  41.8 1.7 %copy-start = (f32[16,16,256]{2,1,0:T(8,128)S(1)}, f32[16,16,256]{2,1,0:T(8,128)}, u32[]{:S(2)}) copy-start(f32[16,16,256]{2,1,0:T(8,128)} %get-tuple-element.5) | copy-start | bytes 786436

commit v3 on v2

--- a/solution.py
+++ b/solution.py
@@ -93,17 +93,11 @@
                 y_down(G.at[planes, pl.ds(0, 8)], GR.at[1, planes])]
 
     def zero_planes(lo):
-        for buf in (T, C, D, M, V, G, B1, Q):
+        for buf in (T, C, D, G):
             buf[pl.ds(lo, X0)] = jnp.zeros((X0, YE, nz), jnp.float32)
 
     pl.when(jnp.logical_not(has_xl))(lambda: zero_planes(0))
     pl.when(jnp.logical_not(has_xu))(lambda: zero_planes(X1))
-
-    def below(k):
-        return jnp.where(has_xl, X0 - k, X0)
-
-    def above(k):
-        return jnp.where(has_xu, X1 + k, X1)
 
     def column(side, part, x, n, first):
         line = HB[side, part, pl.ds(x, 1), :].astype(jnp.float32)
@@ -143,9 +137,10 @@
 
     hx = [x_up(HB.at[1, 1], HB.at[0, 1]), x_down(HB.at[1, 1], HB.at[2, 1])]
     hy = [y_up(HB.at[1, 1], HB.at[1, 0]), y_down(HB.at[1, 1], HB.at[1, 2])]
-    py = packed_links(pl.ds(X0, nx))
+    half = nx // 2
+    py, pz = packed_links(pl.ds(X0, half)), packed_links(pl.ds(X0 + half, nx - half))
     tx, cx, dx = x_links(T, 3), x_links(C, 2), x_links(D, 1)
-    for c in hx + hy + tx + py + cx + dx:
+    for c in hx + hy + py + tx + pz + cx + dx:
         c.start()
 
     keep = (row8 >= jnp.where(has_yu, 0, 4)) & (row8 < jnp.where(has_yl, 8, 4))
@@ -165,6 +160,28 @@
         def _(i):
             f(i)
 
+    def pairs(lo, hi, value, store):
+        @pl.loop(0, (hi - lo) // 2)
+        def _(j):
+            i = lo + 2 * j
+            a, b = value(i), value(i + 1)
+            store(i, a)
+            store(i + 1, b)
+
+    def ends(k, e, value, store):
+        @pl.loop(0, k + e)
+        def _(j):
+            i, n = X0 - k + j, X1 - e + j
+            a, b = value(i), value(n)
+            store(i, a)
+            store(n, b)
+
+    def clear(buf, k):
+        def zero(lo):
+            buf[pl.ds(lo, k)] = jnp.zeros((k, YE, nz), jnp.float32)
+        pl.when(jnp.logical_not(has_xl))(lambda: zero(X0 - k))
+        pl.when(jnp.logical_not(has_xu))(lambda: zero(X1))
+
     lane = lax.broadcasted_iota(jnp.int32, (YE, 128), 1)
 
     def z_up(v):
@@ -183,7 +200,7 @@
         dst[i, rows, :] = v[:ny]
         dst[i, beyond, :] = jnp.where(keep, v[ny:], 0.0)
 
-    def hjb(src, dst, lo, hi, out=None):
+    def hjb(src):
         def f(i):
             v = src[i]
             lap = -6.0 * v
@@ -192,11 +209,18 @@
                          (z_up(v), z_low(v))):
                 lap = lap + (u + l)
                 ham = ham + jnp.square(jnp.maximum(v - l, 0.0)) + jnp.square(jnp.minimum(u - v, 0.0))
-            new = v + DT_HJB * (NU_HJB * lap - 0.5 * ham + C[i])
-            put(dst, i, new)
-            if out is not None:
-                out[i - X0] = new[:ny]
-        loop(lo, hi, f)
+            return v + DT_HJB * (NU_HJB * lap - 0.5 * ham + C[i])
+        return f
+
+    def put_mid(i, v):
+        put(M, i, v)
+
+    def put_halo(i, v):
+        put(V, i, v)
+
+    def put_value(i, v):
+        put(V, i, v)
+        v_out[i - X0] = v[:ny]
 
     def flux(v, vu, m, mu):
         s = v - vu
@@ -205,8 +229,8 @@
     def x_flux(i):
         return flux(V[i, rows, :], V[i + 1, rows, :], D[i, rows, :], D[i + 1, rows, :])
 
-    def transport(lo, hi):
-        def f(i, before):
+    def transport(starts, n):
+        def one(i, before):
             v, m = V[i], D[i]
             fy = flux(v, pltpu.roll(v, YE - 1, 0), m, pltpu.roll(m, YE - 1, 0))
             ly = pltpu.roll(fy, 1, 0)[:ny]
@@ -214,9 +238,14 @@
             fz = flux(v, z_up(v), m, z_up(m))
             lz = z_low(fz, jnp.minimum(-v[:, :128], 0.0) * m[:, :128])
             fx = x_flux(i)
-            G[i, rows, :] = m - DT_FP * ((fx - before) + (fy[:ny] - ly) + (fz - lz))
-            return fx
-        lax.fori_loop(lo, hi, f, x_flux(lo - 1))
+            return fx, m - DT_FP * ((fx - before) + (fy[:ny] - ly) + (fz - lz))
+
+        def f(j, before):
+            done = [one(lo + j, b) for lo, b in zip(starts, before)]
+            for lo, d in zip(starts, done):
+                G[lo + j, rows, :] = d[1]
+            return tuple(d[0] for d in done)
+        lax.fori_loop(0, n, f, tuple(x_flux(lo - 1) for lo in starts))
 
     def beyond_obstacles(side, x, i):
         col = jnp.where(lax.broadcasted_iota(jnp.int32, (8, 1), 0) < 4,
@@ -225,10 +254,17 @@
 
     for c in hy + py:
         c.wait_recv()
-    loop(X0, X1, unpack)
-    hjb(T, M, X0 + 1, X1 - 1)
-    hjb(M, V, X0 + 2, X1 - 2, v_out)
-    transport(X0 + 3, X1 - 3)
+    loop(X0, X0 + half, unpack)
+    pairs(X0 + 1, X0 + half - 1, hjb(T), put_mid)
+    for c in pz:
+        c.wait_recv()
+    loop(X0 + half, X1, unpack)
+    pairs(X0 + half - 1, X1 - 1, hjb(T), put_mid)
+    pairs(X0 + 2, X1 - 2, hjb(M), put_value)
+    transport((X0 + 3, X0 + half), half - 3)
+    gi = field_links(pl.ds(X0 + 3, nx - 6))
+    for c in gi:
+        c.start()
     loop(0, nx, lambda x: beyond_obstacles(1, x, X0 + x))
 
     for c in hx + tx + cx:
@@ -246,17 +282,16 @@
         c.wait_recv()
     for side, has, lo in corners:
         loop(lo, lo + 2, unpack)
-    hjb(T, M, below(2), X0 + 1)
-    hjb(T, M, X1 - 1, above(2))
-    hjb(M, V, below(1), X0)
-    hjb(M, V, X1, above(1))
-    hjb(M, V, X0, X0 + 2, v_out)
-    hjb(M, V, X1 - 2, X1, v_out)
-    transport(X0, X0 + 3)
-    transport(X1 - 3, X1)
+    ends(2, 1, hjb(T), put_mid)
+    clear(M, 2)
+    ends(0, 2, hjb(M), put_value)
+    for i in (X0 - 1, X1):
+        put_halo(i, hjb(M)(i))
+    clear(V, 1)
+    transport((X0, X1 - 3), 3)
 
     gx = x_links(G, 4)
-    gy = field_links(pl.ds(X0, nx))
+    gy = field_links(pl.ds(X0, 3)) + field_links(pl.ds(X1 - 3, 3))
     for c in gx + gy:
         c.start()
 
@@ -272,28 +307,27 @@
     def merge(i):
         G[i, beyond, :] = join(GR[0, i], GR[1, i])
 
-    def shifted(src, i):
-        v = src[i]
-        return v, D4[i] * v - ((src[i + 1] + src[i - 1]) + (pltpu.roll(v, YE - 1, 0) + pltpu.roll(v, 1, 0))
-                               + (z_up(v) + z_low(v)))
+    def shifted(src):
+        def f(i):
+            v = src[i]
+            return D4[i] * v - ((src[i + 1] + src[i - 1]) + (pltpu.roll(v, YE - 1, 0) + pltpu.roll(v, 1, 0))
+                                + (z_up(v) + z_low(v)))
+        return f
 
     R = M
 
-    def first(lo, hi):
-        def f(i):
-            v, b = shifted(G, i)
-            put(R, i, (1.0 - SHIFT) * v - b)
-        loop(lo, hi, f)
-
-    def power(src, dst, lo, hi):
-        loop(lo, hi, lambda i: put(dst, i, shifted(src, i)[1]))
-
-    for c in gy:
+    def residual(i):
+        return (1.0 - SHIFT) * G[i] - shifted(G)(i)
+
+    def into(dst):
+        return lambda i, v: put(dst, i, v)
+
+    for c in gi + gy:
         c.wait_recv()
     loop(X0, X1, merge)
-    first(X0 + 1, X1 - 1)
-    power(R, B1, X0 + 2, X1 - 2)
-    power(B1, Q, X0 + 3, X1 - 3)
+    pairs(X0 + 1, X1 - 1, residual, into(R))
+    pairs(X0 + 2, X1 - 2, shifted(R), into(B1))
+    pairs(X0 + 3, X1 - 3, shifted(B1), into(Q))
 
     for c in gx:
         c.wait_recv()
@@ -304,12 +338,12 @@
         c.wait_recv()
     loop(1, X0, merge)
     loop(X1, X1 + 3, merge)
-    first(below(3), X0 + 1)
-    first(X1 - 1, above(3))
-    power(R, B1, below(2), X0 + 2)
-    power(R, B1, X1 - 2, above(2))
-    power(B1, Q, X0, X0 + 3)
-    power(B1, Q, X1 - 3, above(1))
+    ends(3, 1, residual, into(R))
+    clear(R, 3)
+    ends(2, 2, shifted(R), into(B1))
+    clear(B1, 2)
+    ends(1, 3, shifted(B1), into(Q))
+    clear(Q, 1)
 
     def moments(i, sums):
         r, b = R[i, rows, :], B1[i, rows, :]
@@ -331,6 +365,8 @@
     tile = zero
     for k, s in enumerate(sums):
         tile = jnp.where(tile_row == k, jnp.sum(s, axis=0, keepdims=True), tile)
+    tile = jnp.sum(tile, axis=1, keepdims=True)
+    tile = jnp.sum(jnp.where(tile_row == lane[:8], tile, 0.0), axis=0, keepdims=True)
 
     def all_sum(slots, value, n, me, device, send, recv):
         slots[me] = value
@@ -350,8 +386,7 @@
 
     ca, tile = all_sum(PA, tile, nby, by, lambda j: (bx, j), asend, arecv)
     cb, tile = all_sum(PB, tile, nbx, bx, lambda j: (j, by), bsend, brecv)
-    tile = jnp.broadcast_to(jnp.sum(tile, axis=1, keepdims=True), (8, 128))
-    nu = [tile[k:k + 1] for k in range(6)]
+    nu = [jnp.broadcast_to(tile[:, k:k + 1], (1, 128)) for k in range(6)]
 
     def dot(p, q, s):
         total = 0.0
@@ -389,13 +424,13 @@
     def _(i):
         s_out[i - X0] = G[i, rows, :] + x[0] * R[i, rows, :] + x[1] * B1[i, rows, :] + x[2] * Q[i, rows, :]
 
-    for c in hx + hy + tx + py + cx + dx + pc + gx + gy + gc:
+    for c in hx + hy + tx + py + pz + cx + dx + pc + gx + gi + gy + gc:
         c.wait_send()
     for c in ca + cb:
         c.wait_send()
 
 
-LINKS = 32
+LINKS = 40
 
 
 def per_device(nbx, nby, t, m, p, h):
@@ -410,13 +445,13 @@
         out_specs=(pl.BlockSpec(memory_space=pltpu.VMEM),) * 2,
         scratch_shapes=[ext] * 9 + [
             pltpu.VMEM((nx, ny, nz), jnp.float32), pltpu.VMEM((3, 3, nx, ny), jnp.int32), packed, packed, packed,
-            pltpu.VMEM((nby, 8, 128), jnp.float32), pltpu.VMEM((nbx, 8, 128), jnp.float32),
+            pltpu.VMEM((nby, 1, 128), jnp.float32), pltpu.VMEM((nbx, 1, 128), jnp.float32),
             pltpu.SemaphoreType.DMA((LINKS,)), pltpu.SemaphoreType.DMA((LINKS,)),
             pltpu.SemaphoreType.DMA((nby - 1,)), pltpu.SemaphoreType.DMA((nby - 1,)),
             pltpu.SemaphoreType.DMA((nbx - 1,)), pltpu.SemaphoreType.DMA((nbx - 1,)),
             pltpu.SemaphoreType.DMA((4,)),
         ],
-        compiler_params=pltpu.CompilerParams(collective_id=0, has_side_effects=True),
+        compiler_params=pltpu.CompilerParams(collective_id=0, has_side_effects=True, vmem_limit_bytes=56_000_000),
         name="mean_field_step",
     )(t, m, p, h)
 

time: 44.4 us -> 38.1 us (0.86)
  Pallas kernels: 41.1 us -> 35.1 us
    pallas_call x1, Pallas kernels: 41.1 us -> 35.1 us  [per_device(): pl.pallas_call(functools.partial(kernel, nbx, nby), out_shape=(out, out),...]
where the time goes in v3:
time: 38.1 us; the launch traced here: 37.9 us
  Pallas kernels  35.1 us (92%)
  local copies, waits for them, and re-layouts  2.1 us (6%)
  between operations  0.65 us (2%)
    pallas_call x1, Pallas kernels, per_device(): pl.pallas_call(functools.partial(kernel, nbx, nby), out_shape=(out, out),...  35.1 us
    unnamed x4, local copies, waits for them, and re-layouts  2.1 us

profile of v3, /device:TPU:0, one launch (start us, length us, event | category | flops | bytes accessed | tf_op | source)
XLA Modules:
  0.0 37.9 jit_solution(2387528752724638357)
XLA Ops:
  0.6 0.0 copy-start
  0.6 0.7 %copy-done = s32[16,16]{1,0:T(8,128)S(1)} copy-done((s32[16,16]{1,0:T(8,128)S(1)}, s32[16,16]{1,0:T(8,128)}, u32[]{:S(2)}) %copy-start) | copy-done | bytes 1048
  1.3 35.1 %mean_field_step.1 = (f32[16,16,256]{2,1,0:T(8,128)S(1)}, f32[16,16,256]{2,1,0:T(8,128)S(1)}) custom-call(f32[16,16,256]{2,1,0:T(8,128)} %t_in.1, f32[16,16,256]{2,1,0:T(8,128)} %m_in.1, f32[16,16,256]{2,1,0:T(8,128)} %p_in.1, s32[16,16]{1,0:T(8,128)S(1)} %copy-done), custom_call_target="tpu_custom_call" | custom-call | tf_op jit(solution)/shard_map/mean_field_step/pallas_call | solution.py:441
  36.5 0.7 %copy.8 = f32[16,16,256]{2,1,0:T(8,128)} copy(f32[16,16,256]{2,1,0:T(8,128)S(1)} %get-tuple-element.4) | data formatting | bytes 524288
  37.2 0.7 %copy.9 = f32[16,16,256]{2,1,0:T(8,128)} copy(f32[16,16,256]{2,1,0:T(8,128)S(1)} %get-tuple-element.5) | data formatting | bytes 524288
Async XLA Ops:
  0.6 0.7 %copy-start = (s32[16,16]{1,0:T(8,128)S(1)}, s32[16,16]{1,0:T(8,128)}, u32[]{:S(2)}) copy-start(s32[16,16]{1,0:T(8,128)} %h_in.1) | copy-start | bytes 3076

commit v4 on v3

--- a/solution.py
+++ b/solution.py
@@ -156,9 +156,12 @@
         D[i, beyond, :] = join(pltpu.roll(a, 5, 0), pltpu.roll(b, 3, 0))
 
     def loop(lo, hi, f):
-        @pl.loop(lo, hi)
-        def _(i):
-            f(i)
+        step = 4 if (hi - lo) % 4 == 0 else 1
+
+        @pl.loop(0, (hi - lo) // step)
+        def _(j):
+            for k in range(step):
+                f(lo + step * j + k)
 
     def pairs(lo, hi, value, store):
         @pl.loop(0, (hi - lo) // 2)
@@ -261,12 +264,6 @@
     loop(X0 + half, X1, unpack)
     pairs(X0 + half - 1, X1 - 1, hjb(T), put_mid)
     pairs(X0 + 2, X1 - 2, hjb(M), put_value)
-    transport((X0 + 3, X0 + half), half - 3)
-    gi = field_links(pl.ds(X0 + 3, nx - 6))
-    for c in gi:
-        c.start()
-    loop(0, nx, lambda x: beyond_obstacles(1, x, X0 + x))
-
     for c in hx + tx + cx:
         c.wait_recv()
     corners = ((0, has_xl, X0 - 2), (2, has_xu, X1))
@@ -278,6 +275,12 @@
         pc.append(y_down(HB.at[side, 1], HB.at[side, 2], has))
     for c in pc:
         c.start()
+    transport((X0 + 3, X0 + half), half - 3)
+    gi = field_links(pl.ds(X0 + 3, nx - 6))
+    for c in gi:
+        c.start()
+    loop(0, nx, lambda x: beyond_obstacles(1, x, X0 + x))
+
     for c in dx + pc:
         c.wait_recv()
     for side, has, lo in corners:
@@ -322,18 +325,38 @@
     def into(dst):
         return lambda i, v: put(dst, i, v)
 
+    def moments(i, sums):
+        r, b = R[i, rows, :], B1[i, rows, :]
+        full = Q[i]
+        yu = pltpu.roll(full, YE - 1, 0)[:ny]
+        q = full[:ny]
+        image = D4[i, rows, :] * q - 2.0 * (Q[i + 1, rows, :] + yu + z_up(q))
+        terms = (r * r, r * b, b * b, b * q, q * q, q * image)
+
+        def fold(a):
+            a = a.reshape(ny // 8, 8, nz).sum(axis=0)
+            return sum(a[:, j:j + 128] for j in range(0, nz, 128))
+
+        return tuple(s + fold(a) for s, a in zip(sums, terms))
+
     for c in gi + gy:
         c.wait_recv()
     loop(X0, X1, merge)
     pairs(X0 + 1, X1 - 1, residual, into(R))
     pairs(X0 + 2, X1 - 2, shifted(R), into(B1))
-    pairs(X0 + 3, X1 - 3, shifted(B1), into(Q))
-
     for c in gx:
         c.wait_recv()
     gc = field_links(pl.ds(1, 3)) + field_links(pl.ds(X1, 3))
     for c in gc:
         c.start()
+    pairs(X0 + 3, X1 - 3, shifted(B1), into(Q))
+
+    def two(j, sums):
+        return moments(X0 + 4 + 2 * j, moments(X0 + 3 + 2 * j, sums))
+
+    zero = jnp.zeros((8, 128), jnp.float32)
+    sums = lax.fori_loop(0, (nx - 8) // 2, two, (zero,) * 6)
+
     for c in gc:
         c.wait_recv()
     loop(1, X0, merge)
@@ -345,22 +368,12 @@
     ends(1, 3, shifted(B1), into(Q))
     clear(Q, 1)
 
-    def moments(i, sums):
-        r, b = R[i, rows, :], B1[i, rows, :]
-        full = Q[i]
-        yu = pltpu.roll(full, YE - 1, 0)[:ny]
-        q = full[:ny]
-        image = D4[i, rows, :] * q - 2.0 * (Q[i + 1, rows, :] + yu + z_up(q))
-        terms = (r * r, r * b, b * b, b * q, q * q, q * image)
-
-        def fold(a):
-            a = a.reshape(ny // 8, 8, nz).sum(axis=0)
-            return sum(a[:, j:j + 128] for j in range(0, nz, 128))
-
-        return tuple(s + fold(a) for s, a in zip(sums, terms))
-
-    zero = jnp.zeros((8, 128), jnp.float32)
-    sums = lax.fori_loop(X0, X1, moments, (zero,) * 6)
+    def rest(j, sums):
+        for k in (2 * j, 2 * j + 1):
+            sums = moments(X0 + k + jnp.where(k >= 3, nx - 8, 0), sums)
+        return sums
+
+    sums = lax.fori_loop(0, 4, rest, sums)
     tile_row = lax.broadcasted_iota(jnp.int32, (8, 128), 0)
     tile = zero
     for k, s in enumerate(sums):
@@ -420,9 +433,10 @@
         rr = new
     x = [jnp.concatenate([c] * (nz // 128), axis=1) for c in x]
 
-    @pl.loop(X0, X1)
-    def _(i):
+    def finish(i):
         s_out[i - X0] = G[i, rows, :] + x[0] * R[i, rows, :] + x[1] * B1[i, rows, :] + x[2] * Q[i, rows, :]
+
+    loop(X0, X1, finish)
 
     for c in hx + hy + tx + py + pz + cx + dx + pc + gx + gi + gy + gc:
         c.wait_send()

time: 38.1 us -> 34.3 us (0.900)
  Pallas kernels: 35.1 us -> 31.4 us
    pallas_call x1, Pallas kernels: 35.1 us -> 31.4 us  [per_device(): pl.pallas_call(functools.partial(kernel, nbx, nby), out_shape=(out, out),...]
where the time goes in v4:
time: 34.3 us; the launch traced here: 34.1 us
  Pallas kernels  31.4 us (92%)
  local copies, waits for them, and re-layouts  2.1 us (6%)
  between operations  0.65 us (2%)
    pallas_call x1, Pallas kernels, per_device(): pl.pallas_call(functools.partial(kernel, nbx, nby), out_shape=(out, out),...  31.4 us
    unnamed x4, local copies, waits for them, and re-layouts  2.1 us

profile of v4, /device:TPU:0, one launch (start us, length us, event | category | flops | bytes accessed | tf_op | source)
XLA Modules:
  0.0 34.1 jit_solution(4221636209662817235)
XLA Ops:
  0.6 0.0 copy-start
  0.6 0.7 %copy-done = s32[16,16]{1,0:T(8,128)S(1)} copy-done((s32[16,16]{1,0:T(8,128)S(1)}, s32[16,16]{1,0:T(8,128)}, u32[]{:S(2)}) %copy-start) | copy-done | bytes 1048
  1.3 31.4 %mean_field_step.1 = (f32[16,16,256]{2,1,0:T(8,128)S(1)}, f32[16,16,256]{2,1,0:T(8,128)S(1)}) custom-call(f32[16,16,256]{2,1,0:T(8,128)} %t_in.1, f32[16,16,256]{2,1,0:T(8,128)} %m_in.1, f32[16,16,256]{2,1,0:T(8,128)} %p_in.1, s32[16,16]{1,0:T(8,128)S(1)} %copy-done), custom_call_target="tpu_custom_call" | custom-call | tf_op jit(solution)/shard_map/mean_field_step/pallas_call | solution.py:455
  32.7 0.7 %copy.8 = f32[16,16,256]{2,1,0:T(8,128)} copy(f32[16,16,256]{2,1,0:T(8,128)S(1)} %get-tuple-element.4) | data formatting | bytes 524288
  33.4 0.7 %copy.9 = f32[16,16,256]{2,1,0:T(8,128)} copy(f32[16,16,256]{2,1,0:T(8,128)S(1)} %get-tuple-element.5) | data formatting | bytes 524288
Async XLA Ops:
  0.6 0.7 %copy-start = (s32[16,16]{1,0:T(8,128)S(1)}, s32[16,16]{1,0:T(8,128)}, u32[]{:S(2)}) copy-start(s32[16,16]{1,0:T(8,128)} %h_in.1) | copy-start | bytes 3076
